TPU v7x, 32 devices: a whole 2x2x4 slice. The times are simulated.
32 devices in a mesh: ctx: 8 (over z, x), shard: 4 (over y, core).
Axes of the slice: x: 2, y: 2, z: 4, core: 2. Of those that a mesh axis runs over, the one named last changes fastest.
Arguments:
- token_ids: int32 [4, 2048], P('shard', 'ctx'), may hold values from 0 to 31999
- targets: int32 [4, 2048], P('shard', 'ctx'), may hold values from 0 to 31999
- positions: int32 [4, 2048], P('shard', 'ctx'), may hold values from 0 to 1023, as said below
- embed_table: float32 [32000, 576], P(('ctx', 'shard')), may hold values from -0.52 to 0.52
- projection_weight: float32 [2, 576, 960], P(None, 'shard'), may hold values from -0.25 to 0.25
- w_out: float32 [2, 576, 576], P(None, 'shard'), may hold values from -1 to 1
- w_gate_up: float32 [2, 576, 3072], P(None, 'shard'), may hold values from -0.25 to 0.25
- w_down: float32 [2, 1536, 576], P(None, 'shard'), may hold values from -0.15625 to 0.15625
- norm_gains: float32 [5, 576], P(None, 'shard'), may hold values from 0.5 to 1.5
- table_mom: float32 [32000, 576], P(('ctx', 'shard')), may hold values from -3.0517578e-05 to 3.0517578e-05
- projection_momentum: float32 [2, 576, 960], P(None, 'shard'), may hold values from -0.00018310547 to 0.00018310547
- out_mom: float32 [2, 576, 576], P(None, 'shard'), may hold values from -0.00018310547 to 0.00018310547
- gate_up_mom: float32 [2, 576, 3072], P(None, 'shard'), may hold values from -0.00018310547 to 0.00018310547
- down_mom: float32 [2, 1536, 576], P(None, 'shard'), may hold values from -0.00018310547 to 0.00018310547
- gain_mom: float32 [5, 576], P(None, 'shard'), may hold values from -0.0029296875 to 0.0029296875
- table_avg: float32 [32000, 576], P(('ctx', 'shard')), may hold values from -0.48 to 0.48
- projection_average: float32 [2, 576, 960], P(None, 'shard'), may hold values from -0.25 to 0.25
- out_avg: float32 [2, 576, 576], P(None, 'shard'), may hold values from -1 to 1
- gate_up_avg: float32 [2, 576, 3072], P(None, 'shard'), may hold values from -0.25 to 0.25
- down_avg: float32 [2, 1536, 576], P(None, 'shard'), may hold values from -0.15625 to 0.15625
- gain_avg: float32 [5, 576], P(None, 'shard'), may hold values from 0.5 to 1.5
Outputs:
- mean_loss: float32 [], replicated
- grad_norm: float32 [], replicated
- new_table: float32 [32000, 576], P(('ctx', 'shard'))
- new_qkv: float32 [2, 576, 960], P(None, 'shard')
- new_out: float32 [2, 576, 576], P(None, 'shard')
- new_gate_up: float32 [2, 576, 3072], P(None, 'shard')
- new_down: float32 [2, 1536, 576], P(None, 'shard')
- new_gains: float32 [5, 576], P(None, 'shard')
- table_mom_new: float32 [32000, 576], P(('ctx', 'shard'))
- qkv_mom_new: float32 [2, 576, 960], P(None, 'shard')
- out_mom_new: float32 [2, 576, 576], P(None, 'shard')
- gate_up_mom_new: float32 [2, 576, 3072], P(None, 'shard')
- down_mom_new: float32 [2, 1536, 576], P(None, 'shard')
- gain_mom_new: float32 [5, 576], P(None, 'shard')
- table_avg_new: float32 [32000, 576], P(('ctx', 'shard'))
- qkv_avg_new: float32 [2, 576, 960], P(None, 'shard')
- out_avg_new: float32 [2, 576, 576], P(None, 'shard')
- gate_up_avg_new: float32 [2, 576, 3072], P(None, 'shard')
- down_avg_new: float32 [2, 1536, 576], P(None, 'shard')
- gain_avg_new: float32 [5, 576], P(None, 'shard')
Inputs may be any that keep to these rules, and one draw needn't show every extreme that they name: `positions`: each sequence is a run of whole documents; a token's value counts the tokens before it in its own document, so every document begins with 0. No document is longer than 1024 tokens, and every sequence holds one of exactly 1024 tokens.
All inputs are finite; a program needn't handle non-finite values.
Results may differ from a plain program's by a relative error of at most 0.003.
The roundings to bfloat16 on the way count: a program that leaves them out, or rounds other values in their place, can miss the bound.
Values may be sent and summed in bfloat16 or wider, within the bound.
No kernel may reach another device: no remote copies, remote signals or barrier semaphores. Data moves between devices by JAX's collectives and lax.ppermute only.
A program may use at most 256 MiB of HBM per device.

v0:
```python
import math

import jax
import jax.numpy as jnp
from jax import lax
from jax.sharding import PartitionSpec as P

MODEL_WIDTH = 576
QUERY_HEADS = 9
KEY_VALUE_HEADS = 3
HEAD_SIZE = 64
FF = 1536
V = 32000
LAYER_COUNT = 2
KEYS_PER_BLOCK = 512


SMOOTH = 0.1
Z_WEIGHT = 0.0001
CLIP_NORM = 0.08
LEARN_RATE = 100.0
MOMENTUM = 0.5
AVG_DECAY = 0.5
SCORE_SCALE = 0.125
HIDDEN_SCORE = -1e30
EPSILON = 1e-05
HALF_TYPE = jnp.bfloat16
WIDE_NUMBER_TYPE = jnp.float32


def combined_all(shard, axis, combine):
    everything = jax.tree.map(lambda part: lax.all_gather(part, axis), shard)
    first = jax.tree.map(lambda part: part[0], everything)

    def step(k, so_far):
        return combine(so_far, jax.tree.map(lambda part: part[k], everything))

    return lax.fori_loop(1, lax.axis_size(axis), step, first)


def normed(values, gain_row):
    return (
        values * lax.rsqrt(jnp.mean(values * values, axis=-1, keepdims=True) + EPSILON) * gain_row
    )


def rotary(position_row):
    half_dim = HEAD_SIZE // 2
    inv_freq = 10000.0 ** (-jnp.arange(half_dim, dtype=jnp.float32) / half_dim)
    angles = position_row.astype(jnp.float32)[:, None, None] * inv_freq
    return (jnp.cos(angles), jnp.sin(angles))


def rotary_apply(values, cosine_table, sine_values):
    half_dim = HEAD_SIZE // 2
    first_half = values[..., :half_dim]
    second = values[..., half_dim:]
    return jnp.concatenate(
        [
            first_half * cosine_table - second * sine_values,
            second * cosine_table + first_half * sine_values,
        ],
        axis=-1,
    )


def rotate_back(grads_in, cosine_table, sine_values):
    half_dim = HEAD_SIZE // 2
    first_half = grads_in[..., :half_dim]
    second = grads_in[..., half_dim:]
    return jnp.concatenate(
        [
            first_half * cosine_table + second * sine_values,
            second * cosine_table - first_half * sine_values,
        ],
        axis=-1,
    )


def swiglu(gate_up):
    return jax.nn.silu(gate_up[:, :FF]) * gate_up[:, FF:]


def contract(left_side, right_side, left_dim, right_dim):
    return lax.dot_general(
        left_side,
        right_side,
        (((left_dim,), (right_dim,)), ((), ())),
        preferred_element_type=WIDE_NUMBER_TYPE,
    )


def masked_scores(query_four, key_block, block_start, query_position, document_begin):
    scores = (
        jnp.einsum("qgrd,kgd->grqk", query_four, key_block, preferred_element_type=WIDE_NUMBER_TYPE)
        * SCORE_SCALE
    )
    key_index = block_start + jnp.arange(key_block.shape[0])
    visible = (key_index[None, :] <= query_position[:, None]) & (
        key_index[None, :] >= document_begin[:, None]
    )
    return (scores, visible)


def block_setup(every_key, every_value, query_position, document_begin):
    block_count = every_key.shape[0] // KEYS_PER_BLOCK
    key_block_list = every_key.reshape(block_count, KEYS_PER_BLOCK, KEY_VALUE_HEADS, HEAD_SIZE)
    value_block_list = every_value.reshape(block_count, KEYS_PER_BLOCK, KEY_VALUE_HEADS, HEAD_SIZE)
    starts = jnp.arange(block_count) * KEYS_PER_BLOCK
    first_key = jnp.min(document_begin)
    last_key = jnp.max(query_position)

    def active(block_start):
        return (block_start <= last_key) & (block_start + KEYS_PER_BLOCK - 1 >= first_key)

    return (block_count, key_block_list, value_block_list, starts, active)


def attend_forward(query_four, every_key, every_value, query_position, document_begin):
    token_rows = query_four.shape[0]
    head_groups = QUERY_HEADS // KEY_VALUE_HEADS
    block_count, key_block_list, value_block_list, starts, active = block_setup(
        every_key, every_value, query_position, document_begin
    )

    def stat_step(carry, block_item):
        key_block, block_start = block_item

        def stat_update(carry_state):
            run_max, run_sum = carry_state
            scores, visible = masked_scores(
                query_four, key_block, block_start, query_position, document_begin
            )
            scores = jnp.where(visible, scores, HIDDEN_SCORE)
            new_max = jnp.maximum(run_max, jnp.max(scores, axis=-1))
            exp_terms = jnp.where(visible, jnp.exp(scores - new_max[..., None]), 0.0)
            return (new_max, run_sum * jnp.exp(run_max - new_max) + jnp.sum(exp_terms, axis=-1))

        return (
            lax.cond(active(block_start), stat_update, lambda kept_state: kept_state, carry),
            None,
        )

    start_state = (
        jnp.full((KEY_VALUE_HEADS, head_groups, token_rows), HIDDEN_SCORE, WIDE_NUMBER_TYPE),
        jnp.zeros((KEY_VALUE_HEADS, head_groups, token_rows), WIDE_NUMBER_TYPE),
    )
    (run_max, run_sum), _ = lax.scan(stat_step, start_state, (key_block_list, starts))
    log_total = run_max + jnp.log(run_sum)

    def out_step(carry, block_item):
        key_block, value_block, block_start = block_item

        def out_update(total_out):
            scores, visible = masked_scores(
                query_four, key_block, block_start, query_position, document_begin
            )
            attn_prob = jnp.where(visible, jnp.exp(scores - log_total[..., None]), 0.0)
            return total_out + jnp.einsum(
                "grqk,kgd->qgrd",
                attn_prob.astype(HALF_TYPE),
                value_block,
                preferred_element_type=WIDE_NUMBER_TYPE,
            )

        return (lax.cond(active(block_start), out_update, lambda kept_out: kept_out, carry), None)

    attended_output, _ = lax.scan(
        out_step,
        jnp.zeros((token_rows, KEY_VALUE_HEADS, head_groups, HEAD_SIZE), WIDE_NUMBER_TYPE),
        (key_block_list, value_block_list, starts),
    )
    return (attended_output, log_total)


def attend_backward(
    query_four, every_key, every_value, log_total, grad_four, query_position, document_begin
):
    token_rows = query_four.shape[0]
    head_groups = QUERY_HEADS // KEY_VALUE_HEADS
    block_count, key_block_list, value_block_list, starts, active = block_setup(
        every_key, every_value, query_position, document_begin
    )

    def probs_and_grads(key_block, value_block, block_start):
        scores, visible = masked_scores(
            query_four, key_block, block_start, query_position, document_begin
        )
        attn_prob = jnp.where(visible, jnp.exp(scores - log_total[..., None]), 0.0)
        grad_prob = jnp.einsum(
            "qgrd,kgd->grqk", grad_four, value_block, preferred_element_type=WIDE_NUMBER_TYPE
        )
        return (attn_prob, grad_prob)

    def delta_step(carry, block_item):
        key_block, value_block, block_start = block_item

        def delta_update(delta_sum):
            attn_prob, grad_prob = probs_and_grads(key_block, value_block, block_start)
            return delta_sum + jnp.sum(attn_prob * grad_prob, axis=-1)

        return (lax.cond(active(block_start), delta_update, lambda kept_sum: kept_sum, carry), None)

    delta_sum, _ = lax.scan(
        delta_step,
        jnp.zeros((KEY_VALUE_HEADS, head_groups, token_rows), WIDE_NUMBER_TYPE),
        (key_block_list, value_block_list, starts),
    )

    def grad_step(carry, block_item):
        key_block, value_block, block_start = block_item

        def grad_update(query_gradient):
            attn_prob, grad_prob = probs_and_grads(key_block, value_block, block_start)
            grad_score = (attn_prob * (grad_prob - delta_sum[..., None])).astype(HALF_TYPE)
            query_gradient = (
                query_gradient
                + jnp.einsum(
                    "grqk,kgd->qgrd", grad_score, key_block, preferred_element_type=WIDE_NUMBER_TYPE
                )
                * SCORE_SCALE
            )
            key_gradient = (
                jnp.einsum(
                    "grqk,qgrd->kgd",
                    grad_score,
                    query_four,
                    preferred_element_type=WIDE_NUMBER_TYPE,
                )
                * SCORE_SCALE
            )
            value_gradient = jnp.einsum(
                "grqk,qgrd->kgd",
                attn_prob.astype(HALF_TYPE),
                grad_four,
                preferred_element_type=WIDE_NUMBER_TYPE,
            )
            return (
                query_gradient,
                jnp.concatenate(
                    [
                        key_gradient.reshape(KEYS_PER_BLOCK, KEY_VALUE_HEADS * HEAD_SIZE),
                        value_gradient.reshape(KEYS_PER_BLOCK, KEY_VALUE_HEADS * HEAD_SIZE),
                    ],
                    axis=1,
                ),
            )

        def skip_block(query_gradient):
            return (
                query_gradient,
                jnp.zeros((KEYS_PER_BLOCK, 2 * KEY_VALUE_HEADS * HEAD_SIZE), WIDE_NUMBER_TYPE),
            )

        return lax.cond(active(block_start), grad_update, skip_block, carry)

    query_gradient, gradient_block_list = lax.scan(
        grad_step,
        jnp.zeros((token_rows, KEY_VALUE_HEADS, head_groups, HEAD_SIZE), WIDE_NUMBER_TYPE),
        (key_block_list, value_block_list, starts),
    )
    return (
        query_gradient,
        gradient_block_list.reshape(block_count * KEYS_PER_BLOCK, 2 * KEY_VALUE_HEADS * HEAD_SIZE),
    )


def advance(weight, grad_one, moment, average, factor):
    clipped = grad_one * factor
    moment_new = MOMENTUM * moment + clipped
    weight_new = weight - LEARN_RATE * (clipped + MOMENTUM * moment_new)
    return (weight_new, moment_new, AVG_DECAY * average + (1.0 - AVG_DECAY) * weight_new)


def shards(
    token_ids,
    targets,
    positions,
    embed_table,
    projection_weight,
    w_out,
    w_gate_up,
    w_down,
    norm_gains,
    table_mom,
    projection_momentum,
    out_mom,
    gate_up_mom,
    down_mom,
    gain_mom,
    table_avg,
    projection_average,
    out_avg,
    gate_up_avg,
    down_avg,
    gain_avg,
):
    ctx_count = lax.axis_size("ctx")
    shard_count = lax.axis_size("shard")
    ctx_index = lax.axis_index("ctx")
    shard_index = lax.axis_index("shard")
    token_rows = token_ids.shape[1]
    own_rows = embed_table.shape[0]
    group_rows = shard_count * token_rows
    all_tokens = group_rows * ctx_count
    head_groups = QUERY_HEADS // KEY_VALUE_HEADS
    query_span_width = QUERY_HEADS * HEAD_SIZE
    key_value_width = KEY_VALUE_HEADS * HEAD_SIZE
    vocab_slice = lax.all_gather(embed_table.astype(HALF_TYPE), "ctx", axis=0, tiled=True)
    slice_rows = vocab_slice.shape[0]
    group_ids, group_targets = (
        lax.all_gather(token_ids, "shard", axis=0, tiled=True),
        lax.all_gather(targets, "shard", axis=0, tiled=True),
    )
    group_ids = group_ids.reshape(group_rows)
    group_targets = group_targets.reshape(group_rows)

    def locate(vocab_id):
        owner_shard = vocab_id // own_rows % shard_count
        local_row = vocab_id // (own_rows * shard_count) * own_rows + vocab_id % own_rows
        return (owner_shard == shard_index, local_row)

    id_here, id_row = locate(group_ids)
    target_here, target_row = locate(group_targets)
    picked = jnp.where(id_here[:, None], vocab_slice[id_row].astype(WIDE_NUMBER_TYPE), 0.0)
    hidden = lax.psum_scatter(
        picked.astype(jnp.bfloat16), "shard", scatter_dimension=0, tiled=True
    ).astype(jnp.float32)
    position_row = positions[0]
    cosine_table, sine_values = rotary(position_row)
    query_position = ctx_index * token_rows + jnp.arange(token_rows)
    document_begin = query_position - position_row

    def fetch_layer(layer_id):
        return (
            lax.all_gather(
                projection_weight[layer_id].astype(HALF_TYPE), "shard", axis=0, tiled=True
            ),
            lax.all_gather(w_out[layer_id].astype(HALF_TYPE), "shard", axis=0, tiled=True),
            lax.all_gather(w_gate_up[layer_id].astype(HALF_TYPE), "shard", axis=0, tiled=True),
            lax.all_gather(w_down[layer_id].astype(HALF_TYPE), "shard", axis=0, tiled=True),
            lax.all_gather(norm_gains.astype(HALF_TYPE), "shard", axis=1, tiled=True),
        )

    saved_state = []
    for layer_id in range(LAYER_COUNT):
        fetched = fetch_layer(layer_id)
        qkv_full, out_full, gate_up_full, down_full, gain_full = fetched
        gain_values = gain_full.astype(WIDE_NUMBER_TYPE)
        layer_input = hidden
        attn_in = normed(hidden, gain_values[2 * layer_id]).astype(HALF_TYPE)
        projected_rows = jnp.dot(attn_in, qkv_full, preferred_element_type=WIDE_NUMBER_TYPE)
        query_four = (
            rotary_apply(
                projected_rows[:, :query_span_width].reshape(token_rows, QUERY_HEADS, HEAD_SIZE),
                cosine_table,
                sine_values,
            )
            .astype(HALF_TYPE)
            .reshape(token_rows, KEY_VALUE_HEADS, head_groups, HEAD_SIZE)
        )
        key_rows = (
            rotary_apply(
                projected_rows[:, query_span_width : query_span_width + key_value_width].reshape(
                    token_rows, KEY_VALUE_HEADS, HEAD_SIZE
                ),
                cosine_table,
                sine_values,
            )
            .astype(HALF_TYPE)
            .reshape(token_rows, key_value_width)
        )
        value_rows = projected_rows[:, query_span_width + key_value_width :].astype(HALF_TYPE)
        every_key, every_value = (
            lax.all_gather(key_rows, "ctx", axis=0, tiled=True),
            lax.all_gather(value_rows, "ctx", axis=0, tiled=True),
        )
        attended_output, log_total = attend_forward(
            query_four, every_key, every_value, query_position, document_begin
        )
        attn_out = attended_output.reshape(token_rows, query_span_width).astype(HALF_TYPE)
        hidden = hidden + jnp.dot(attn_out, out_full, preferred_element_type=WIDE_NUMBER_TYPE)
        middle = hidden
        mlp_in = normed(hidden, gain_values[2 * layer_id + 1]).astype(HALF_TYPE)
        gate_up = jnp.dot(mlp_in, gate_up_full, preferred_element_type=WIDE_NUMBER_TYPE)
        hidden = hidden + jnp.dot(
            swiglu(gate_up).astype(HALF_TYPE), down_full, preferred_element_type=WIDE_NUMBER_TYPE
        )
        saved_state.append(
            (layer_input, middle, query_four, every_key, every_value, log_total, attn_out, None)
        )
    final_gain = gain_values[2 * LAYER_COUNT]
    final_half = normed(hidden, final_gain).astype(HALF_TYPE)
    group_final = lax.all_gather(final_half, "shard", axis=0, tiled=True)
    row_block = math.gcd(512, group_rows)
    n_row_blocks = group_rows // row_block
    hidden_blocks = group_final.reshape(n_row_blocks, row_block, MODEL_WIDTH)
    target_blocks = target_row.reshape(n_row_blocks, row_block)
    here_blocks = target_here.reshape(n_row_blocks, row_block)

    def stat_block(block_item):
        hidden_block, target_block, here_block = block_item
        logits = contract(hidden_block, vocab_slice, 1, 1)
        row_max = jnp.max(logits, axis=-1)
        exp_sum = jnp.sum(jnp.exp(logits - row_max[:, None]), axis=-1)
        chosen = jnp.take_along_axis(logits, target_block[:, None], axis=1)[:, 0]
        return (row_max, exp_sum, jnp.sum(logits, axis=-1), jnp.where(here_block, chosen, 0.0))

    stat_parts = lax.map(stat_block, (hidden_blocks, target_blocks, here_blocks))
    row_max, exp_sum, logit_sum, target_logit = [
        stat_part.reshape(group_rows) for stat_part in stat_parts
    ]

    def combine(first_stats, second_stats):
        max_a, sum_a, logit_a, target_a = first_stats
        max_b, sum_b, logit_b, target_b = second_stats
        joint_max = jnp.maximum(max_a, max_b)
        return (
            joint_max,
            sum_a * jnp.exp(max_a - joint_max) + sum_b * jnp.exp(max_b - joint_max),
            logit_a + logit_b,
            target_a + target_b,
        )

    row_max, exp_sum, logit_sum, target_logit = combined_all(
        (row_max, exp_sum, logit_sum, target_logit), "shard", combine
    )
    row_lse = row_max + jnp.log(exp_sum)
    token_loss = (
        row_lse
        - (1.0 - SMOOTH) * target_logit
        - SMOOTH * logit_sum / V
        + Z_WEIGHT * row_lse * row_lse
    )
    own_loss = (
        jnp.sum(lax.dynamic_slice_in_dim(token_loss, shard_index * token_rows, token_rows))
        / all_tokens
    )
    lse_blocks = row_lse.reshape(n_row_blocks, row_block)
    slice_index = jnp.arange(slice_rows)

    def grad_block(slice_grad, block_item):
        hidden_block, target_block, here_block, lse_block = block_item
        logits = contract(hidden_block, vocab_slice, 1, 1)
        onehot = ((slice_index[None, :] == target_block[:, None]) & here_block[:, None]).astype(
            WIDE_NUMBER_TYPE
        )
        grad_logits = (
            jnp.exp(logits - lse_block[:, None]) * (1.0 + 2.0 * Z_WEIGHT * lse_block[:, None])
            - (1.0 - SMOOTH) * onehot
            - SMOOTH / V
        ) / all_tokens
        grad_half = grad_logits.astype(HALF_TYPE)
        return (
            slice_grad + contract(grad_half, hidden_block, 0, 0),
            jnp.dot(grad_half, vocab_slice, preferred_element_type=WIDE_NUMBER_TYPE),
        )

    slice_grad, hidden_grad_blocks = lax.scan(
        grad_block,
        jnp.zeros((slice_rows, MODEL_WIDTH), WIDE_NUMBER_TYPE),
        (hidden_blocks, target_blocks, here_blocks, lse_blocks),
    )
    hidden_grad = lax.psum_scatter(
        hidden_grad_blocks.reshape(group_rows, MODEL_WIDTH),
        "shard",
        scatter_dimension=0,
        tiled=True,
    )
    _, final_back = jax.vjp(normed, hidden, final_gain)
    grad_hidden, grad_final_gain = final_back(hidden_grad)
    layer_grads = [None] * LAYER_COUNT
    for layer_id in reversed(range(LAYER_COUNT)):
        (
            layer_input,
            middle,
            query_four,
            every_key,
            every_value,
            log_total,
            attn_out,
            kept_weights,
        ) = saved_state[layer_id]
        qkv_full, out_full, gate_up_full, down_full, gain_full = fetch_layer(layer_id)
        gain_values = gain_full.astype(WIDE_NUMBER_TYPE)
        mlp_float, mlp_back = jax.vjp(normed, middle, gain_values[2 * layer_id + 1])
        mlp_in = mlp_float.astype(HALF_TYPE)
        gate_up = jnp.dot(mlp_in, gate_up_full, preferred_element_type=WIDE_NUMBER_TYPE)
        act_float, act_back = jax.vjp(swiglu, gate_up)
        act_half = act_float.astype(HALF_TYPE)
        out_grad = grad_hidden.astype(HALF_TYPE)
        grad_down = contract(act_half, out_grad, 0, 0)
        grad_act = contract(out_grad, down_full, 1, 1)
        grad_gate_up = act_back(grad_act)[0].astype(HALF_TYPE)
        grad_gu_weight = contract(mlp_in, grad_gate_up, 0, 0)
        grad_middle, grad_gain_mlp = mlp_back(contract(grad_gate_up, gate_up_full, 1, 1))
        grad_hidden = grad_hidden + grad_middle
        branch_grad = grad_hidden.astype(HALF_TYPE)
        grad_out_weight = contract(attn_out, branch_grad, 0, 0)
        grad_attended = (
            contract(branch_grad, out_full, 1, 1)
            .astype(HALF_TYPE)
            .reshape(token_rows, KEY_VALUE_HEADS, head_groups, HEAD_SIZE)
        )
        query_gradient, grad_kv_rows = attend_backward(
            query_four,
            every_key,
            every_value,
            log_total,
            grad_attended,
            query_position,
            document_begin,
        )
        key_value_gradient = lax.psum_scatter(grad_kv_rows, "ctx", scatter_dimension=0, tiled=True)
        attn_float, attn_back = jax.vjp(normed, layer_input, gain_values[2 * layer_id])
        attn_in = attn_float.astype(HALF_TYPE)
        grad_projected = jnp.concatenate(
            [
                rotate_back(
                    query_gradient.reshape(token_rows, QUERY_HEADS, HEAD_SIZE),
                    cosine_table,
                    sine_values,
                ).reshape(token_rows, query_span_width),
                rotate_back(
                    key_value_gradient[:, :key_value_width].reshape(
                        token_rows, KEY_VALUE_HEADS, HEAD_SIZE
                    ),
                    cosine_table,
                    sine_values,
                ).reshape(token_rows, key_value_width),
                key_value_gradient[:, key_value_width:],
            ],
            axis=1,
        ).astype(HALF_TYPE)
        grad_qkv_weight = contract(attn_in, grad_projected, 0, 0)
        grad_input, grad_gain_attn = attn_back(contract(grad_projected, qkv_full, 1, 1))
        grad_hidden = grad_hidden + grad_input
        gain_rows = (
            jnp.zeros((2 * LAYER_COUNT + 1, MODEL_WIDTH), WIDE_NUMBER_TYPE)
            .at[2 * layer_id]
            .set(grad_gain_attn)
            .at[2 * layer_id + 1]
            .set(grad_gain_mlp)
        )
        if layer_id == LAYER_COUNT - 1:
            gain_rows = gain_rows.at[2 * LAYER_COUNT].set(grad_final_gain)
        grad_set = (grad_qkv_weight, grad_out_weight, grad_gu_weight, grad_down, gain_rows)
        shard_grads = (
            lax.psum_scatter(grad_set[0], "shard", scatter_dimension=0, tiled=True),
            lax.psum_scatter(grad_set[1], "shard", scatter_dimension=0, tiled=True),
            lax.psum_scatter(grad_set[2], "shard", scatter_dimension=0, tiled=True),
            lax.psum_scatter(grad_set[3], "shard", scatter_dimension=0, tiled=True),
            lax.psum_scatter(grad_set[4], "shard", scatter_dimension=1, tiled=True),
        )
        layer_grads[layer_id] = lax.psum(
            (shard_grads[0], shard_grads[1], shard_grads[2], shard_grads[3], shard_grads[4]), "ctx"
        )
    all_grads = lax.all_gather(grad_hidden, "shard", axis=0, tiled=True)
    slice_grad = slice_grad.at[id_row].add(jnp.where(id_here[:, None], all_grads, 0.0))
    table_grad = lax.psum_scatter(slice_grad, "ctx", scatter_dimension=0, tiled=True)
    qkv_grad = jnp.stack([layer_grads[layer_no][0] for layer_no in range(LAYER_COUNT)])
    out_grad_all = jnp.stack([layer_grads[layer_no][1] for layer_no in range(LAYER_COUNT)])
    gate_up_grad = jnp.stack([layer_grads[layer_no][2] for layer_no in range(LAYER_COUNT)])
    down_grad = jnp.stack([layer_grads[layer_no][3] for layer_no in range(LAYER_COUNT)])
    gain_grad = layer_grads[0][4]
    layer_no = 1
    gain_grad = gain_grad + layer_grads[layer_no][4]
    layer_square = sum(
        (
            jnp.sum(grad_one * grad_one)
            for grad_one in (qkv_grad, out_grad_all, gate_up_grad, down_grad, gain_grad)
        )
    )
    loss_sum, square_sum = lax.psum(
        (own_loss, layer_square / ctx_count + jnp.sum(table_grad * table_grad)), ("ctx", "shard")
    )
    grad_norm = jnp.sqrt(square_sum)
    factor = CLIP_NORM / jnp.maximum(grad_norm, CLIP_NORM)
    table_new = advance(embed_table, table_grad, table_mom, table_avg, factor)
    qkv_new = advance(projection_weight, qkv_grad, projection_momentum, projection_average, factor)
    out_new = advance(w_out, out_grad_all, out_mom, out_avg, factor)
    gate_up_new = advance(w_gate_up, gate_up_grad, gate_up_mom, gate_up_avg, factor)
    down_new = advance(w_down, down_grad, down_mom, down_avg, factor)
    gains_new = advance(norm_gains, gain_grad, gain_mom, gain_avg, factor)
    return (
        loss_sum,
        grad_norm,
        table_new[0],
        qkv_new[0],
        out_new[0],
        gate_up_new[0],
        down_new[0],
        gains_new[0],
        table_new[1],
        qkv_new[1],
        out_new[1],
        gate_up_new[1],
        down_new[1],
        gains_new[1],
        table_new[2],
        qkv_new[2],
        out_new[2],
        gate_up_new[2],
        down_new[2],
        gains_new[2],
    )


def solution(mesh):
    return jax.shard_map(
        shards,
        mesh=mesh,
        in_specs=(
            P("shard", "ctx"),
            P("shard", "ctx"),
            P("shard", "ctx"),
            P(("ctx", "shard"), None),
            P(None, "shard", None),
            P(None, "shard", None),
            P(None, "shard", None),
            P(None, "shard", None),
            P(None, "shard"),
            P(("ctx", "shard"), None),
            P(None, "shard", None),
            P(None, "shard", None),
            P(None, "shard", None),
            P(None, "shard", None),
            P(None, "shard"),
            P(("ctx", "shard"), None),
            P(None, "shard", None),
            P(None, "shard", None),
            P(None, "shard", None),
            P(None, "shard", None),
            P(None, "shard"),
        ),
        out_specs=(
            P(),
            P(),
            P(("ctx", "shard"), None),
            P(None, "shard", None),
            P(None, "shard", None),
            P(None, "shard", None),
            P(None, "shard", None),
            P(None, "shard"),
            P(("ctx", "shard"), None),
            P(None, "shard", None),
            P(None, "shard", None),
            P(None, "shard", None),
            P(None, "shard", None),
            P(None, "shard"),
            P(("ctx", "shard"), None),
            P(None, "shard", None),
            P(None, "shard", None),
            P(None, "shard", None),
            P(None, "shard", None),
            P(None, "shard"),
        ),
        check_vma=False,
    )
```

profile of v0, /device:TPU:0, one launch (start us, length us, event | category | flops | bytes accessed | tf_op | source)
XLA Modules:
  0.0 2194.5 jit_solution(14669358923992957024)
XLA Ops:
  17.0 133.8 %all-gather.42.cloned.1.call-done = bf16[8,1000,576]{1,2,0:T(8,128)(2,1)} async-done(((bf16[1,1000,576]{1,2,0:T(8,128)(2,1)}), bf16[8,1000,576]{1,2,0:T(8,128)(2,1)}) %all-gather.42.cloned.1.call-update) | async-done | bytes 9216016 | tf_op jit(solution)/shard_map/all_gather | solution.py:309
  150.8 14.2 copy.198
  164.9 9.4 gather_fusion.1
  191.8 12.2 all-gather.1
  214.2 9.6 all-gather.30.cloned.1.call-done
  227.6 32.3 %all_gather.81 = bf16[2048,192]{0,1:T(8,128)(2,1)S(1)} all-gather(bf16[256,192]{0,1:T(8,128)(2,1)S(1)} %bitcast.559), channel_id=1, replica_groups=mesh['ctx'=8,'shard'=4] {'ctx'}, dimensions={0}, use_global_device_ids=true | all-gather | bytes 884736 | tf_op jit(solution)/shard_map/all_gather | solution.py:375
  260.7 18.4 while.205
  279.1 34.2 %all_gather.82 = bf16[2048,192]{0,1:T(8,128)(2,1)S(1)} all-gather(bf16[256,192]{0,1:T(8,128)(2,1)S(1)} %copy-done.84), channel_id=1, replica_groups=mesh['ctx'=8,'shard'=4] {'ctx'}, dimensions={0}, use_global_device_ids=true | all-gather | bytes 884736 | tf_op jit(solution)/shard_map/all_gather | solution.py:376
  315.1 19.3 while.206
  347.0 35.9 %all_gather.87 = bf16[2048,192]{0,1:T(8,128)(2,1)S(1)} all-gather(bf16[256,192]{0,1:T(8,128)(2,1)S(1)} %bitcast.560), channel_id=1, replica_groups=mesh['ctx'=8,'shard'=4] {'ctx'}, dimensions={0}, use_global_device_ids=true | all-gather | bytes 884736 | tf_op jit(solution)/shard_map/all_gather | solution.py:375
  383.7 32.6 %all_gather.88 = bf16[2048,192]{0,1:T(8,128)(2,1)S(1)} all-gather(bf16[256,192]{0,1:T(8,128)(2,1)S(1)} %slice.415), channel_id=1, replica_groups=mesh['ctx'=8,'shard'=4] {'ctx'}, dimensions={0}, use_global_device_ids=true | all-gather | bytes 884736 | tf_op jit(solution)/shard_map/all_gather | solution.py:376
  420.0 18.4 while.207
  439.3 19.6 while.208
  477.2 23.3 %all-gather.26.cloned.1.call-done = bf16[1024,576]{0,1:T(8,128)(2,1)} async-done(((bf16[256,576]{0,1:T(8,128)(2,1)}), bf16[1024,576]{0,1:T(8,128)(2,1)}) %all-gather.26.cloned.1.call-update) | async-done | bytes 1179664 | tf_op jit(solution)/shard_map/all_gather | solution.py:394
  502.2 59.6 %while.203 = (s32[]{:T(128)}, f32[2,512]{1,0:T(2,128)S(1)}, f32[2,512]{1,0:T(2,128)S(1)}, f32[2,512]{1,0:T(2,128)S(1)}, f32[2,512]{1,0:T(2,128)S(1)}, /*index=5*...) while((s32[]{:T(128)}, f32[2,512]{1,0:T(2,128)S(1)}, ...), condition=%wide.region_32.33_spmd, body=%wide.region_28.32_spmd.sunk | while | flops 4734983680 | bytes 42699400 | solution.py:409
  502.2 14.0 fusion.301
  531.9 14.1 fusion.301
  583.6 130.7 %while.213 = (s32[]{:T(128)}, f32[8000,576]{0,1:T(8,128)}, f32[2,512,576]{1,0,2:T(2,128)}, bf16[2,512,576]{2,1,0:T(8,128)(2,1)S(1)}, bf16[8000,576]{1,0:T(8,128)...) while((s32[]{:T(128)}, f32[8000,576]{0,1:T(8,128)}, ...), condition=%wide.region_38.39_spmd.clone, body=%wide.region_37.38_spmd.clone.sunk | while | flops 14201857024 | bytes 87101064 | solution.py:459
  583.8 16.2 multiply_convert_fusion.14
  600.0 11.3 select_add_fusion.2
  611.3 12.7 convolution_bitcast_fusion.4
  625.2 21.8 dynamic_update_slice.57
  647.1 16.2 multiply_convert_fusion.14
  663.3 15.1 select_add_fusion.2
  678.3 12.7 convolution_bitcast_fusion.4
  692.3 21.8 dynamic_update_slice.57
  718.0 33.0 %reduce-scatter.21.cloned.1.call-done = f32[256,576]{0,1:T(8,128)} async-done(((f32[1024,576]{0,1:T(8,128)}), f32[256,576]{0,1:T(8,128)}) %reduce-scatter.21.cloned.1.call-update) | async-done | bytes 589840 | tf_op jit(solution)/shard_map/reduce_scatter | solution.py:464
  761.9 19.7 while.209
  783.5 28.2 %while.210 = (s32[]{:T(128)}, f32[256,3,3,64]{0,3,2,1:T(8,128)S(1)}, f32[4,512,384]{2,1,0:T(8,128)}, s32[4]{0:T(128)}, s32[]{:T(128)}, /*index=5*/s32[]{:T(128)}...) while((s32[]{:T(128)}, f32[256,3,3,64]{0,3,2,1:T(8,128)S(1)}, ...), condition=%wide.region_50.51_spmd.clone, body=%wide.region_47.50_spmd.clone.sunk | while | flops 767755008 | bytes 30119240 | solution.py:257
  812.6 96.3 %reduce-scatter.23.cloned.1.call-done = f32[256,384]{1,0:T(8,128)} async-done(((f32[2048,384]{1,0:T(8,128)}), f32[256,384]{1,0:T(8,128)}) %reduce-scatter.23.cloned.1.call-update) | async-done | bytes 393232 | tf_op jit(solution)/shard_map/reduce_scatter | solution.py:514
  920.7 19.7 while.211
  942.4 28.2 %while.212 = (s32[]{:T(128)}, f32[256,3,3,64]{0,3,2,1:T(8,128)S(1)}, f32[4,512,384]{2,1,0:T(8,128)}, s32[4]{0:T(128)}, s32[]{:T(128)}, /*index=5*/s32[]{:T(128)}...) while((s32[]{:T(128)}, f32[256,3,3,64]{0,3,2,1:T(8,128)S(1)}, ...), condition=%wide.region_62.63_spmd.clone, body=%wide.region_59.62_spmd.clone.sunk | while | flops 767755008 | bytes 30119240 | solution.py:257
  992.1 75.4 %reduce-scatter.25.cloned.1.call-done = f32[256,384]{1,0:T(8,128)} async-done(((f32[2048,384]{1,0:T(8,128)}), f32[256,384]{1,0:T(8,128)}) %reduce-scatter.25.cloned.1.call-update) | async-done | bytes 393232 | tf_op jit(solution)/shard_map/reduce_scatter | solution.py:514
  1082.8 13.9 reduce-scatter.33.cloned.1.call-done
  1096.7 43.3 %reduce-scatter.41.cloned.1.call-done = f32[384,576]{0,1:T(8,128)} async-done(((f32[1536,576]{0,1:T(8,128)}), f32[384,576]{0,1:T(8,128)}) %reduce-scatter.41.cloned.1.call-update) | async-done | bytes 884752 | tf_op jit(solution)/shard_map/reduce_scatter | solution.py:552
  1139.9 30.4 %reduce-scatter.31.cloned.1.call-done = f32[144,576]{1,0:T(8,128)} async-done(((f32[576,576]{1,0:T(8,128)}), f32[144,576]{1,0:T(8,128)}) %reduce-scatter.31.cloned.1.call-update) | async-done | bytes 331792 | tf_op jit(solution)/shard_map/reduce_scatter | solution.py:550
  1170.4 35.8 %reduce-scatter.29.cloned.1.call-done = f32[144,960]{1,0:T(8,128)} async-done(((f32[576,960]{1,0:T(8,128)}), f32[144,960]{1,0:T(8,128)}) %reduce-scatter.29.cloned.1.call-update) | async-done | bytes 552976 | tf_op jit(solution)/shard_map/reduce_scatter | solution.py:549
  1206.2 43.2 %reduce-scatter.39.cloned.1.call-done = f32[384,576]{0,1:T(8,128)} async-done(((f32[1536,576]{0,1:T(8,128)}), f32[384,576]{0,1:T(8,128)}) %reduce-scatter.39.cloned.1.call-update) | async-done | bytes 884752 | tf_op jit(solution)/shard_map/reduce_scatter | solution.py:552
  1249.4 66.6 %reduce-scatter.37.cloned.1.call-done = f32[144,3072]{1,0:T(8,128)} async-done(((f32[576,3072]{1,0:T(8,128)}), f32[144,3072]{1,0:T(8,128)}) %reduce-scatter.37.cloned.1.call-update) | async-done | bytes 1769488 | tf_op jit(solution)/shard_map/reduce_scatter | solution.py:551
  1316.0 36.0 %reduce-scatter.27.cloned.1.call-done = f32[144,960]{1,0:T(8,128)} async-done(((f32[576,960]{1,0:T(8,128)}), f32[144,960]{1,0:T(8,128)}) %reduce-scatter.27.cloned.1.call-update) | async-done | bytes 552976 | tf_op jit(solution)/shard_map/reduce_scatter | solution.py:549
  1352.0 66.6 %reduce-scatter.35.cloned.1.call-done = f32[144,3072]{1,0:T(8,128)} async-done(((f32[576,3072]{1,0:T(8,128)}), f32[144,3072]{1,0:T(8,128)}) %reduce-scatter.35.cloned.1.call-update) | async-done | bytes 1769488 | tf_op jit(solution)/shard_map/reduce_scatter | solution.py:551
  1418.6 20.2 copy.224
  1450.3 20.9 scatter_fusion
  1481.1 23.3 %psum.96 = f32[5,144]{1,0:T(8,128)S(1)} all-reduce(f32[5,144]{1,0:T(8,128)S(1)} %copy.259), channel_id=1, replica_groups=mesh['ctx'=8,'shard'=4] {'ctx'}, use_global_device_ids=true, to_apply=%region_87.88 | all-reduce | flops 720 | bytes 5760 | tf_op jit(solution)/shard_map/psum | solution.py:555
  1505.0 206.5 %all-reduce.11.cloned.1.call-done = (f32[1,144,960]{2,1,0:T(8,128)}, f32[1,144,960]{2,1,0:T(8,128)}, f32[1,144,576]{2,1,0:T(8,128)}, f32[1,144,576]{2,1,0:T(8,12...) async-done(((f32[1,144,960]{2,1,0:T(8,128)}, f32[1,144,960]{2,1,0:T(8,128)}, f32[1,144,576]{2,1,0:T(8,128)}, ...) | async-done | bytes 7077904 | tf_op jit(solution)/shard_map/psum | solution.py:555
  1730.0 366.4 %reduce-scatter.45.cloned.1.call-done = f32[1000,576]{1,0:T(8,128)} async-done(((f32[8000,576]{1,0:T(8,128)}), f32[1000,576]{1,0:T(8,128)}) %reduce-scatter.45.cloned.1.call-update) | async-done | bytes 2304016
  2103.2 42.7 %all-reduce.7 = (f32[]{:T(128)}, f32[]{:T(128)}) all-reduce(f32[]{:T(128)S(6)} %div.161, f32[]{:T(128)S(6)} %add.858), channel_id=1, replica_groups=mesh['ctx'=8,'shard'=4] {'ctx','shard'}, use_global_device_ids=true, to_apply=%region_36.37 | all-reduce | flops 2 | bytes 16 | tf_op jit(solution)/shard_map/psum | solution.py:574
  2170.9 10.0 add_multiply_fusion
  (749 shorter events, 401.3 us)
Async XLA Ops:
  7.2 143.6 %all-gather.42.cloned.1.call-start = ((), (), s32[]{:S(2)}) async-start(), calls=%async_computation.34 | async-start | bytes 10616832 | tf_op jit(solution)/shard_map/all_gather | solution.py:309
  10.1 203.0 %reduce-scatter.19.cloned.1.call-start = ((), (), s32[]{:S(2)}) async-start(), calls=%async_computation.14 | async-start | bytes 1474560 | tf_op jit(solution)/shard_map/reduce_scatter | solution.py:326
  16.4 158.6 %copy-start.118 = (pred[1024]{0:T(1024)(128)(4,1)}, pred[1024]{0:T(1024)(128)(4,1)S(1)}, u32[]{:S(2)}) copy-start(pred[1024]{0:T(1024)(128)(4,1)S(1)} %fusion.228) | copy-start | bytes 3076
  176.3 47.5 %all-gather.30.cloned.1.call-start = ((), (), s32[]{:S(2)}) async-start(), calls=%async_computation.28 | async-start | bytes 1474560 | tf_op jit(solution)/shard_map/all_gather | solution.py:336
  178.7 156.6 %all-gather.32.cloned.1.call-start = ((), (), s32[]{:S(2)}) async-start(), calls=%async_computation.29 | async-start | bytes 4423680 | tf_op jit(solution)/shard_map/all_gather | solution.py:340
  180.4 160.9 %all-gather.34.cloned.1.call-start = ((), (), s32[]{:S(2)}) async-start(), calls=%async_computation.30 | async-start | bytes 2211840 | tf_op jit(solution)/shard_map/all_gather | solution.py:341
  182.4 161.4 %all-gather.36.cloned.1.call-start = ((), (), s32[]{:S(2)}) async-start(), calls=%async_computation.31 | async-start | bytes 1474560 | tf_op jit(solution)/shard_map/all_gather | solution.py:336
  183.0 278.3 %all-gather.38.cloned.1.call-start = ((), (), s32[]{:S(2)}) async-start(), calls=%async_computation.32 | async-start | bytes 4423680 | tf_op jit(solution)/shard_map/all_gather | solution.py:340
  183.7 283.5 %all-gather.40.cloned.1.call-start = ((), (), s32[]{:S(2)}) async-start(), calls=%async_computation.33 | async-start | bytes 2211840 | tf_op jit(solution)/shard_map/all_gather | solution.py:341
  184.5 316.0 %all-gather.26.cloned.1.call-start = ((), (), s32[]{:S(2)}) async-start(), calls=%async_computation.15 | async-start | bytes 1474560 | tf_op jit(solution)/shard_map/all_gather | solution.py:394
  191.0 35.0 %copy-start.90 = (f32[576]{0:T(1024)}, f32[576]{0:T(1024)S(1)}, u32[]{:S(2)}) copy-start(f32[576]{0:T(1024)S(1)} %get-tuple-element.3919) | copy-start | bytes 6916
  204.0 130.5 %copy-start.39 = (bf16[1,576,576]{2,1,0:T(8,128)(2,1)}, bf16[1,576,576]{2,1,0:T(8,128)(2,1)S(1)}, u32[]{:S(2)}) copy-start(bf16[1,576,576]{2,1,0:T(8,128)(2,1)S(1)} %all-gather.1) | copy-start | bytes 1990660
  213.1 206.8 %copy-start.59 = (f32[256,32]{0,1:T(8,128)}, f32[256,32]{0,1:T(8,128)S(1)}, u32[]{:S(2)}) copy-start(f32[256,32]{0,1:T(8,128)S(1)} %get-tuple-element.4240) | copy-start | bytes 98308
  213.1 206.8 %copy-start.61 = (f32[256,32]{0,1:T(8,128)}, f32[256,32]{0,1:T(8,128)S(1)}, u32[]{:S(2)}) copy-start(f32[256,32]{0,1:T(8,128)S(1)} %get-tuple-element.4241) | copy-start | bytes 98308
  227.5 33.1 %copy-start.82 = (bf16[256,9,32]{0,2,1:T(8,128)(2,1)S(1)}, bf16[256,9,32]{0,2,1:T(8,128)(2,1)}, u32[]{:S(2)}) copy-start(bf16[256,9,32]{0,2,1:T(8,128)(2,1)} %get-tuple-element.4221) | copy-start | bytes 442372
  227.5 33.1 %copy-start.83 = (bf16[256,9,32]{0,2,1:T(8,128)(2,1)S(1)}, bf16[256,9,32]{0,2,1:T(8,128)(2,1)}, u32[]{:S(2)}) copy-start(bf16[256,9,32]{0,2,1:T(8,128)(2,1)} %get-tuple-element.4222) | copy-start | bytes 442372
  279.1 35.9 %copy-start.65 = (s32[256]{0:T(256)}, s32[256]{0:T(256)S(1)}, u32[]{:S(2)}) copy-start(s32[256]{0:T(256)S(1)} %get-tuple-element.5585) | copy-start | bytes 3076
  343.7 116.8 %copy-start.14 = (f32[256,576]{0,1:T(8,128)}, f32[256,576]{0,1:T(8,128)S(1)}, u32[]{:S(2)}) copy-start(f32[256,576]{0,1:T(8,128)S(1)} %get-tuple-element.4247) | copy-start | bytes 1769476
  383.5 36.4 %slice-start = ((f32[256,960]{0,1:T(8,128)}), f32[256,576]{0,1:T(8,128)S(1)}, s32[]{:S(2)}) async-start(f32[256,960]{0,1:T(8,128)} %copy-done.50), calls=%async_computation.38 | async-start | bytes 1179648 | tf_op jit(solution)/shard_map/slice | solution.py:355
  439.3 21.2 copy-start.41
  471.4 279.7 %reduce-scatter.21.cloned.1.call-start = ((), (), s32[]{:S(2)}) async-start(), calls=%async_computation.16 | async-start | bytes 2949120 | tf_op jit(solution)/shard_map/reduce_scatter | solution.py:464
  714.3 36.8 %copy-start.29 = (f32[256,576]{0,1:T(8,128)S(1)}, f32[256,576]{0,1:T(8,128)}, u32[]{:S(2)}) copy-start(f32[256,576]{0,1:T(8,128)} %copy-done.28) | copy-start | bytes 1769476
  714.3 36.8 %copy-start.95 = (f32[576]{0:T(1024)S(1)}, f32[576]{0:T(1024)}, u32[]{:S(2)}) copy-start(f32[576]{0:T(1024)} %get-tuple-element.3915) | copy-start | bytes 6916
  714.3 36.8 %copy-start.111 = (f32[256]{0:T(256)S(1)}, f32[256]{0:T(256)}, u32[]{:S(2)}) copy-start(f32[256]{0:T(256)} %copy-done.110) | copy-start | bytes 3076
  718.0 35.1 %copy-start.127 = (f32[256]{0:T(256)S(1)}, f32[256]{0:T(256)}, u32[]{:S(2)}) copy-start(f32[256]{0:T(256)} %copy-done.126) | copy-start | bytes 3076
  718.0 36.3 %copy-start.64 = (bf16[1,1536,576]{1,2,0:T(8,128)(2,1)S(1)}, bf16[1,1536,576]{1,2,0:T(8,128)(2,1)}, u32[]{:S(2)}) copy-start(bf16[1,1536,576]{1,2,0:T(8,128)(2,1)} %all-gather.40.cloned.1.call-done) | copy-start | bytes 5308420
  718.0 190.9 %reduce-scatter.23.cloned.1.call-start = ((), (), s32[]{:S(2)}) async-start(), calls=%async_computation.17 | async-start | bytes 3538944 | tf_op jit(solution)/shard_map/reduce_scatter | solution.py:514
  811.7 99.5 %copy-start.15 = (f32[256,576]{0,1:T(8,128)S(1)}, f32[256,576]{0,1:T(8,128)}, u32[]{:S(2)}) copy-start(f32[256,576]{0,1:T(8,128)} %copy-done.14) | copy-start | bytes 1769476
  811.7 99.5 %copy-start.93 = (f32[576]{0:T(1024)S(1)}, f32[576]{0:T(1024)}, u32[]{:S(2)}) copy-start(f32[576]{0:T(1024)} %get-tuple-element.3917) | copy-start | bytes 6916
  811.7 99.5 %copy-start.106 = (f32[256]{0:T(256)S(1)}, f32[256]{0:T(256)}, u32[]{:S(2)}) copy-start(f32[256]{0:T(256)} %copy-done.105) | copy-start | bytes 3076
  811.7 255.8 %reduce-scatter.25.cloned.1.call-start = ((), (), s32[]{:S(2)}) async-start(), calls=%async_computation.18 | async-start | bytes 3538944 | tf_op jit(solution)/shard_map/reduce_scatter | solution.py:514
  812.6 101.3 %copy-start.74 = (bf16[256,9,64]{0,2,1:T(8,128)(2,1)}, bf16[256,9,64]{0,2,1:T(8,128)(2,1)S(1)}, u32[]{:S(2)}) copy-start(bf16[256,9,64]{0,2,1:T(8,128)(2,1)S(1)} %pad_maximum_fusion.4) | copy-start | bytes 884740
  970.6 126.1 %reduce-scatter.33.cloned.1.call-start = ((), (), s32[]{:S(2)}) async-start(), calls=%async_computation.22 | async-start | bytes 1843200 | tf_op jit(solution)/shard_map/reduce_scatter | solution.py:550
  973.2 166.7 %reduce-scatter.41.cloned.1.call-start = ((), (), s32[]{:S(2)}) async-start(), calls=%async_computation.26 | async-start | bytes 4423680 | tf_op jit(solution)/shard_map/reduce_scatter | solution.py:552
  975.8 194.6 %reduce-scatter.31.cloned.1.call-start = ((), (), s32[]{:S(2)}) async-start(), calls=%async_computation.21 | async-start | bytes 1843200 | tf_op jit(solution)/shard_map/reduce_scatter | solution.py:550
  978.4 227.7 %reduce-scatter.29.cloned.1.call-start = ((), (), s32[]{:S(2)}) async-start(), calls=%async_computation.20 | async-start | bytes 2949120 | tf_op jit(solution)/shard_map/reduce_scatter | solution.py:549
  981.7 267.7 %reduce-scatter.39.cloned.1.call-start = ((), (), s32[]{:S(2)}) async-start(), calls=%async_computation.25 | async-start | bytes 4423680 | tf_op jit(solution)/shard_map/reduce_scatter | solution.py:552
  984.2 331.8 %reduce-scatter.37.cloned.1.call-start = ((), (), s32[]{:S(2)}) async-start(), calls=%async_computation.24 | async-start | bytes 8847360 | tf_op jit(solution)/shard_map/reduce_scatter | solution.py:551
  991.2 78.7 %copy-start.31 = (bf16[256,576]{0,1:T(8,128)(2,1)S(1)}, bf16[256,576]{0,1:T(8,128)(2,1)}, u32[]{:S(2)}) copy-start(bf16[256,576]{0,1:T(8,128)(2,1)} %reduce-scatter.19.cloned.1.call-done) | copy-start | bytes 884740
  991.2 78.7 %copy-start.91 = (f32[576]{0:T(1024)S(1)}, f32[576]{0:T(1024)}, u32[]{:S(2)}) copy-start(f32[576]{0:T(1024)} %copy-done.90) | copy-start | bytes 6916
  991.2 78.7 %copy-start.108 = (f32[256]{0:T(256)S(1)}, f32[256]{0:T(256)}, u32[]{:S(2)}) copy-start(f32[256]{0:T(256)} %copy-done.107) | copy-start | bytes 3076
  991.2 360.7 %reduce-scatter.27.cloned.1.call-start = ((), (), s32[]{:S(2)}) async-start(), calls=%async_computation.19 | async-start | bytes 2949120 | tf_op jit(solution)/shard_map/reduce_scatter | solution.py:549
  1073.0 345.6 %reduce-scatter.35.cloned.1.call-start = ((), (), s32[]{:S(2)}) async-start(), calls=%async_computation.23 | async-start | bytes 8847360 | tf_op jit(solution)/shard_map/reduce_scatter | solution.py:551
  1078.5 366.3 %all-gather.28.cloned.1.call-start = ((), (), s32[]{:S(2)}) async-start(), calls=%async_computation.27 | async-start | bytes 2949120 | tf_op jit(solution)/shard_map/all_gather | solution.py:558
  1081.4 398.8 %reduce-scatter.43.cloned.1.call-start = ((), (), s32[]{:S(2)}) async-start(), calls=%async_computation.35 | async-start | bytes 368640
  1082.7 628.8 %all-reduce.11.cloned.1.call-start = ((), (), s32[]{:S(2)}) async-start(), calls=%async_computation.37 | async-start | bytes 14450688 | tf_op jit(solution)/shard_map/psum | solution.py:555
  1418.6 677.9 %reduce-scatter.45.cloned.1.call-start = ((), (), s32[]{:S(2)}) async-start(), calls=%async_computation.36 | async-start | bytes 23040000
  1418.6 26.2 %copy-start.119 = (pred[1024]{0:T(1024)(128)(4,1)S(1)}, pred[1024]{0:T(1024)(128)(4,1)}, u32[]{:S(2)}) copy-start(pred[1024]{0:T(1024)(128)(4,1)} %copy-done.118) | copy-start | bytes 3076
  (111 other events, 399.1 us)
Sparse Core Ops, SparseCore 0:
  10.8 139.9 all-gather.41
  176.4 27.5 reduce-scatter.18
  206.2 17.5 all-gather.29
  225.8 30.7 all-gather.31
  258.6 20.6 all-gather.33
  281.3 17.4 all-gather.35
  300.9 30.7 all-gather.37
  333.8 20.6 all-gather.39
  471.5 28.9 all-gather.25
  718.1 32.9 reduce-scatter.20
  811.8 96.9 reduce-scatter.22
  970.7 96.8 reduce-scatter.24
  1070.1 26.4 reduce-scatter.32
  1099.7 40.2 reduce-scatter.40
  1142.9 27.3 reduce-scatter.30
  1173.3 32.8 reduce-scatter.28
  1209.2 40.2 reduce-scatter.38
  1251.8 64.1 reduce-scatter.36
  1319.1 32.8 reduce-scatter.26
  1354.3 64.1 reduce-scatter.34
  1420.7 24.0 all-gather.27
  1447.8 20.2 reduce-scatter.42
  1473.5 237.8 all-reduce.10
  1714.9 381.5 reduce-scatter.44
where the time goes:
time: 2210 us; the launch traced here: 2190 us
  waiting for transfers between devices  1290 us (58%)
  blocking collectives  259 us (12%)
  local copies, waits for them, and re-layouts  231 us (10%)
  matrix products  196 us (9%)
  other arithmetic  109 us (5%)
  loops' own time  85.2 us (4%)
  between operations  23.4 us (1%)
    unnamed x26, waiting for transfers between devices  369 us
    psum x1, waiting for transfers between devices, shards(): lax.psum((shard_grads[0], shard_grads[1], shard_grads[2], shard_grads[3],...  206 us
    reduce_scatter x2, waiting for transfers between devices, shards(): lax.psum_scatter(grad_kv_rows, 'ctx', scatter_dimension=0, tiled=True)  172 us
    all_gather x1, waiting for transfers between devices, shards(): lax.all_gather(embed_table.astype(HALF_TYPE), 'ctx', axis=0, tiled=True)  134 us
    reduce_scatter x2, waiting for transfers between devices, shards(): lax.psum_scatter(grad_set[2], 'shard', scatter_dimension=0, tiled=True)  133 us
    dot_general x22, matrix products, contract(): lax.dot_general(left_side, right_side, (((left_dim,), (right_dim,)), ((),...  126 us
    reduce_scatter x2, waiting for transfers between devices, shards(): lax.psum_scatter(grad_set[3], 'shard', scatter_dimension=0, tiled=True)  86.5 us
    reduce_scatter x2, waiting for transfers between devices, shards(): lax.psum_scatter(grad_set[0], 'shard', scatter_dimension=0, tiled=True)  71.8 us
  transfers between devices with their start and end apart: 24, of which 17 were waited for; matrix products, arithmetic and copies ran while one was open for 8% of the time, Pallas kernels for 0%

commit v1 on v0

v1 whole, which is shorter than its diff:
```python
import jax
import jax.numpy as jnp
from jax import lax
from jax.experimental import pallas as pl
from jax.experimental.pallas import tpu as pltpu
from jax.sharding import PartitionSpec as P

MODEL_WIDTH = 576
QUERY_HEADS = 9
KEY_VALUE_HEADS = 3
HEAD_SIZE = 64
FF = 1536
V = 32000
LAYER_COUNT = 2
GROUPS = QUERY_HEADS // KEY_VALUE_HEADS


SMOOTH = 0.1
Z_WEIGHT = 0.0001
CLIP_NORM = 0.08
LEARN_RATE = 100.0
MOMENTUM = 0.5
AVG_DECAY = 0.5
SCORE_SCALE = 0.125
HIDDEN_SCORE = -1e30
EPSILON = 1e-05
HALF_TYPE = jnp.bfloat16
WIDE_NUMBER_TYPE = jnp.float32


def normed(values, gain_row):
    return (
        values * lax.rsqrt(jnp.mean(values * values, axis=-1, keepdims=True) + EPSILON) * gain_row
    )


def rotary(position_row):
    half_dim = HEAD_SIZE // 2
    inv_freq = 10000.0 ** (-jnp.arange(half_dim, dtype=jnp.float32) / half_dim)
    angles = position_row.astype(jnp.float32)[:, None, None] * inv_freq
    return (jnp.cos(angles), jnp.sin(angles))


def rotary_apply(values, cosine_table, sine_values):
    half_dim = HEAD_SIZE // 2
    first_half = values[..., :half_dim]
    second = values[..., half_dim:]
    return jnp.concatenate(
        [
            first_half * cosine_table - second * sine_values,
            second * cosine_table + first_half * sine_values,
        ],
        axis=-1,
    )


def rotate_back(grads_in, cosine_table, sine_values):
    half_dim = HEAD_SIZE // 2
    first_half = grads_in[..., :half_dim]
    second = grads_in[..., half_dim:]
    return jnp.concatenate(
        [
            first_half * cosine_table + second * sine_values,
            second * cosine_table - first_half * sine_values,
        ],
        axis=-1,
    )


def swiglu(gate_up):
    return jax.nn.silu(gate_up[:, :FF]) * gate_up[:, FF:]


def contract(left_side, right_side, left_dim, right_dim):
    return lax.dot_general(
        left_side,
        right_side,
        (((left_dim,), (right_dim,)), ((), ())),
        preferred_element_type=WIDE_NUMBER_TYPE,
    )


def butterfly(values, axis, combine):
    count = lax.axis_size(axis)
    step = 1
    while step < count:
        other = lax.ppermute(values, axis, [(i, i ^ step) for i in range(count)])
        values = combine(values, other)
        step *= 2
    return values


def add_all(values, axes):
    for axis in axes:
        values = butterfly(values, axis, jnp.add)
    return values


def exchange_sum(partial, axis):
    count = lax.axis_size(axis)
    index = lax.axis_index(axis)
    rows = partial.shape[0] // count

    def block(which):
        return lax.dynamic_slice_in_dim(partial, which * rows, rows, axis=0)

    total = block(index)
    for step in range(1, count):
        sent = lax.ppermute(
            block(index ^ step).astype(HALF_TYPE), axis, [(i, i ^ step) for i in range(count)]
        )
        total = total + sent.astype(WIDE_NUMBER_TYPE)
    return total


def window_visible(position_column, key_rows):
    rows = position_column.shape[0]
    base = key_rows - rows
    query_at = lax.broadcasted_iota(jnp.int32, (rows, key_rows), 0) + base
    key_at = lax.broadcasted_iota(jnp.int32, (rows, key_rows), 1)
    return (key_at <= query_at) & (key_at >= query_at - position_column)


def head_slice(head):
    return slice(head * HEAD_SIZE, (head + 1) * HEAD_SIZE)


def attend_kernel(query_ref, key_ref, value_ref, position_ref, out_ref, total_ref):
    key_rows = key_ref.shape[0]
    visible = window_visible(position_ref[...], key_rows)
    for head in range(QUERY_HEADS):
        group = head // GROUPS
        scores = (
            contract(query_ref[:, head_slice(head)], key_ref[:, head_slice(group)], 1, 1)
            * SCORE_SCALE
        )
        scores = jnp.where(visible, scores, HIDDEN_SCORE)
        row_max = jnp.max(scores, axis=1, keepdims=True)
        terms = jnp.exp(scores - row_max)
        row_sum = jnp.sum(terms, axis=1, keepdims=True)
        prob = (terms * (1.0 / row_sum)).astype(HALF_TYPE)
        out_ref[:, head_slice(head)] = contract(
            prob, value_ref[:, head_slice(group)], 1, 0
        ).astype(HALF_TYPE)
        total_ref[:, head : head + 1] = row_max + jnp.log(row_sum)


def attend(query, keys, values, position_column):
    rows = query.shape[0]
    return pl.pallas_call(
        attend_kernel,
        out_shape=(
            jax.ShapeDtypeStruct((rows, QUERY_HEADS * HEAD_SIZE), HALF_TYPE),
            jax.ShapeDtypeStruct((rows, 16), WIDE_NUMBER_TYPE),
        ),
        compiler_params=pltpu.CompilerParams(vmem_limit_bytes=48 << 20),
        name="attend",
    )(query, keys, values, position_column)


def attend_back_kernel(
    query_ref, key_ref, value_ref, total_ref, grad_ref, position_ref, dq_ref, dkv_ref
):
    key_rows = key_ref.shape[0]
    width = KEY_VALUE_HEADS * HEAD_SIZE
    visible = window_visible(position_ref[...], key_rows)
    for group in range(KEY_VALUE_HEADS):
        keys = key_ref[:, head_slice(group)]
        values = value_ref[:, head_slice(group)]
        key_grad = None
        value_grad = None
        for head in range(group * GROUPS, (group + 1) * GROUPS):
            query = query_ref[:, head_slice(head)]
            grad = grad_ref[:, head_slice(head)]
            scores = contract(query, keys, 1, 1) * SCORE_SCALE
            prob = jnp.where(visible, jnp.exp(scores - total_ref[:, head : head + 1]), 0.0)
            grad_prob = contract(grad, values, 1, 1)
            delta = jnp.sum(prob * grad_prob, axis=1, keepdims=True)
            grad_score = (prob * (grad_prob - delta)).astype(HALF_TYPE)
            dq_ref[:, head_slice(head)] = contract(grad_score, keys, 1, 0) * SCORE_SCALE
            key_part = contract(grad_score, query, 0, 0)
            value_part = contract(prob.astype(HALF_TYPE), grad, 0, 0)
            key_grad = key_part if key_grad is None else key_grad + key_part
            value_grad = value_part if value_grad is None else value_grad + value_part
        dkv_ref[:, head_slice(group)] = key_grad * SCORE_SCALE
        dkv_ref[:, width + group * HEAD_SIZE : width + (group + 1) * HEAD_SIZE] = value_grad


def attend_back(query, keys, values, totals, grads, position_column):
    rows = query.shape[0]
    return pl.pallas_call(
        attend_back_kernel,
        out_shape=(
            jax.ShapeDtypeStruct((rows, QUERY_HEADS * HEAD_SIZE), WIDE_NUMBER_TYPE),
            jax.ShapeDtypeStruct(
                (keys.shape[0], 2 * KEY_VALUE_HEADS * HEAD_SIZE), WIDE_NUMBER_TYPE
            ),
        ),
        compiler_params=pltpu.CompilerParams(vmem_limit_bytes=48 << 20),
        name="attend_back",
    )(query, keys, values, totals, grads, position_column)


def stats_kernel(final_ref, target_ref, table_ref, out_ref):
    logits = contract(final_ref[...], table_ref[...], 1, 1)
    row_max = jnp.max(logits, axis=1, keepdims=True)
    exp_sum = jnp.sum(jnp.exp(logits - row_max), axis=1, keepdims=True)
    logit_sum = jnp.sum(logits, axis=1, keepdims=True)
    column = lax.broadcasted_iota(jnp.int32, logits.shape, 1)
    chosen = jnp.sum(jnp.where(column == target_ref[...], logits, 0.0), axis=1, keepdims=True)
    out_ref[:, 0:1] = row_max
    out_ref[:, 1:2] = exp_sum
    out_ref[:, 2:3] = logit_sum
    out_ref[:, 3:4] = chosen


TOKEN_TILE = 256


def vocab_stats(finals, target_column, table_rows):
    tokens = finals.shape[0]
    tile = TOKEN_TILE
    return pl.pallas_call(
        stats_kernel,
        grid=(tokens // tile,),
        in_specs=[
            pl.BlockSpec((tile, MODEL_WIDTH), lambda i: (i, 0)),
            pl.BlockSpec((tile, 1), lambda i: (i, 0)),
            pl.BlockSpec(table_rows.shape, lambda i: (0, 0), pipeline_mode=pl.Buffered(1)),
        ],
        out_specs=pl.BlockSpec((tile, 4), lambda i: (i, 0)),
        out_shape=jax.ShapeDtypeStruct((tokens, 4), WIDE_NUMBER_TYPE),
        compiler_params=pltpu.CompilerParams(vmem_limit_bytes=56 << 20),
        name="vocab_stats",
    )(finals, target_column, table_rows)


def vocab_grad_kernel(all_tokens, final_ref, target_ref, lse_ref, table_ref, dx_ref, dw_ref):
    finals = final_ref[...]
    table = table_ref[...]
    logits = contract(finals, table, 1, 1)
    lse = lse_ref[...]
    column = lax.broadcasted_iota(jnp.int32, logits.shape, 1)
    grad = (
        jnp.exp(logits - lse) * (1.0 + 2.0 * Z_WEIGHT * lse)
        - jnp.where(column == target_ref[...], 1.0 - SMOOTH, 0.0)
        - SMOOTH / V
    ) / all_tokens
    grad = grad.astype(HALF_TYPE)
    dx_ref[...] = contract(grad, table, 1, 0)
    part = contract(grad, finals, 0, 0)

    @pl.when(pl.program_id(0) == 0)
    def _():
        dw_ref[...] = part

    @pl.when(pl.program_id(0) > 0)
    def _():
        dw_ref[...] += part


def vocab_grad(finals, target_column, lse_column, table_rows, all_tokens):
    tokens = finals.shape[0]
    tile = TOKEN_TILE

    def body(*refs):
        vocab_grad_kernel(all_tokens, *refs)

    return pl.pallas_call(
        body,
        grid=(tokens // tile,),
        in_specs=[
            pl.BlockSpec((tile, MODEL_WIDTH), lambda i: (i, 0)),
            pl.BlockSpec((tile, 1), lambda i: (i, 0)),
            pl.BlockSpec((tile, 1), lambda i: (i, 0)),
            pl.BlockSpec(table_rows.shape, lambda i: (0, 0), pipeline_mode=pl.Buffered(1)),
        ],
        out_specs=(
            pl.BlockSpec((tile, MODEL_WIDTH), lambda i: (i, 0)),
            pl.BlockSpec(table_rows.shape, lambda i: (0, 0), pipeline_mode=pl.Buffered(1)),
        ),
        out_shape=(
            jax.ShapeDtypeStruct((tokens, MODEL_WIDTH), WIDE_NUMBER_TYPE),
            jax.ShapeDtypeStruct(table_rows.shape, WIDE_NUMBER_TYPE),
        ),
        compiler_params=pltpu.CompilerParams(vmem_limit_bytes=60 << 20),
        name="vocab_grad",
    )(finals, target_column, lse_column, table_rows)


def advance(weight, grad_one, moment, average, factor):
    clipped = grad_one * factor
    moment_new = MOMENTUM * moment + clipped
    weight_new = weight - LEARN_RATE * (clipped + MOMENTUM * moment_new)
    return (weight_new, moment_new, AVG_DECAY * average + (1.0 - AVG_DECAY) * weight_new)


def shards(
    token_ids,
    targets,
    positions,
    embed_table,
    projection_weight,
    w_out,
    w_gate_up,
    w_down,
    norm_gains,
    table_mom,
    projection_momentum,
    out_mom,
    gate_up_mom,
    down_mom,
    gain_mom,
    table_avg,
    projection_average,
    out_avg,
    gate_up_avg,
    down_avg,
    gain_avg,
):
    ctx_count = lax.axis_size("ctx")
    shard_count = lax.axis_size("shard")
    ctx_index = lax.axis_index("ctx")
    shard_index = lax.axis_index("shard")
    token_rows = token_ids.shape[1]
    own_rows = embed_table.shape[0]
    sequence = token_rows * ctx_count
    all_tokens = sequence * shard_count
    query_span_width = QUERY_HEADS * HEAD_SIZE
    key_value_width = KEY_VALUE_HEADS * HEAD_SIZE
    back = ctx_count // 2

    table_rows = lax.all_gather(embed_table.astype(HALF_TYPE), "shard", axis=0, tiled=True)
    slice_rows = table_rows.shape[0]
    pairs = lax.all_gather(
        jnp.concatenate([token_ids, targets], axis=0), ("ctx", "shard"), axis=0
    ).reshape(ctx_count, shard_count, 2, token_rows)
    every_id = pairs[:, :, 0].reshape(all_tokens)
    sequence_pairs = lax.dynamic_index_in_dim(pairs, shard_index, axis=1, keepdims=False)
    first_row = ctx_index * slice_rows
    id_row = sequence_pairs[:, 0].reshape(sequence) - first_row
    target_column = sequence_pairs[:, 1].reshape(sequence, 1) - first_row
    id_here = (id_row >= 0) & (id_row < slice_rows)
    picked = jnp.where(
        id_here[:, None], table_rows[jnp.where(id_here, id_row, 0)], jnp.zeros((), HALF_TYPE)
    )
    looked_up = lax.all_to_all(
        picked.reshape(ctx_count, token_rows, MODEL_WIDTH), "ctx", 0, 0, tiled=True
    )
    hidden = jnp.sum(looked_up.astype(WIDE_NUMBER_TYPE), axis=0)
    position_row = positions[0]
    position_column = position_row[:, None]
    cosine_table, sine_values = rotary(position_row)
    gain_values = lax.all_gather(
        norm_gains.astype(HALF_TYPE), "shard", axis=1, tiled=True
    ).astype(WIDE_NUMBER_TYPE)

    def gathered(weight, layer_id):
        return lax.all_gather(weight[layer_id].astype(HALF_TYPE), "shard", axis=0, tiled=True)

    fetched = [
        tuple(gathered(weight, layer_id) for weight in (projection_weight, w_out, w_gate_up, w_down))
        for layer_id in range(LAYER_COUNT)
    ]

    saved_state = []
    for layer_id in range(LAYER_COUNT):
        qkv_full, out_full, gate_up_full, down_full = fetched[layer_id]
        layer_input = hidden
        attn_in = normed(hidden, gain_values[2 * layer_id]).astype(HALF_TYPE)
        projected_kv = jnp.dot(
            attn_in, qkv_full[:, query_span_width:], preferred_element_type=WIDE_NUMBER_TYPE
        )
        key_rows = (
            rotary_apply(
                projected_kv[:, :key_value_width].reshape(token_rows, KEY_VALUE_HEADS, HEAD_SIZE),
                cosine_table,
                sine_values,
            )
            .astype(HALF_TYPE)
            .reshape(token_rows, key_value_width)
        )
        own_kv = jnp.concatenate(
            [key_rows, projected_kv[:, key_value_width:].astype(HALF_TYPE)], axis=1
        )
        window = [
            lax.ppermute(own_kv, "ctx", [(i, i + step) for i in range(ctx_count - step)])
            for step in range(back, 0, -1)
        ]
        window_kv = jnp.concatenate(window + [own_kv], axis=0)
        window_keys = window_kv[:, :key_value_width]
        window_values = window_kv[:, key_value_width:]
        projected_query = jnp.dot(
            attn_in, qkv_full[:, :query_span_width], preferred_element_type=WIDE_NUMBER_TYPE
        )
        query = (
            rotary_apply(
                projected_query.reshape(token_rows, QUERY_HEADS, HEAD_SIZE),
                cosine_table,
                sine_values,
            )
            .astype(HALF_TYPE)
            .reshape(token_rows, query_span_width)
        )
        attn_out, log_total = attend(query, window_keys, window_values, position_column)
        hidden = hidden + jnp.dot(attn_out, out_full, preferred_element_type=WIDE_NUMBER_TYPE)
        middle = hidden
        mlp_in = normed(hidden, gain_values[2 * layer_id + 1]).astype(HALF_TYPE)
        gate_up = jnp.dot(mlp_in, gate_up_full, preferred_element_type=WIDE_NUMBER_TYPE)
        act_half = swiglu(gate_up).astype(HALF_TYPE)
        hidden = hidden + jnp.dot(act_half, down_full, preferred_element_type=WIDE_NUMBER_TYPE)
        saved_state.append(
            (
                layer_input,
                middle,
                query,
                window_keys,
                window_values,
                log_total,
                attn_out,
                attn_in,
                mlp_in,
                gate_up,
                act_half,
            )
        )
    final_gain = gain_values[2 * LAYER_COUNT]
    final_half = normed(hidden, final_gain).astype(HALF_TYPE)
    sequence_final = lax.all_gather(final_half, "ctx", axis=0, tiled=True)

    def combine(first_stats, second_stats):
        joint_max = jnp.maximum(first_stats[0], second_stats[0])
        return jnp.stack(
            [
                joint_max,
                first_stats[1] * jnp.exp(first_stats[0] - joint_max)
                + second_stats[1] * jnp.exp(second_stats[0] - joint_max),
                first_stats[2] + second_stats[2],
                first_stats[3] + second_stats[3],
            ]
        )

    stats = vocab_stats(sequence_final, target_column, table_rows).T
    stats = butterfly(stats, "ctx", combine)
    row_lse = stats[0] + jnp.log(stats[1])
    token_loss = (
        row_lse
        - (1.0 - SMOOTH) * stats[3]
        - SMOOTH * stats[2] / V
        + Z_WEIGHT * row_lse * row_lse
    )
    own_loss = (
        jnp.sum(lax.dynamic_slice_in_dim(token_loss, ctx_index * token_rows, token_rows))
        / all_tokens
    )
    hidden_grad_parts, slice_grad = vocab_grad(
        sequence_final, target_column, row_lse[:, None], table_rows, all_tokens
    )
    hidden_grad = lax.psum_scatter(hidden_grad_parts, "ctx", scatter_dimension=0, tiled=True)
    table_grad = exchange_sum(slice_grad, "shard")
    _, final_back = jax.vjp(normed, hidden, final_gain)
    grad_hidden, grad_final_gain = final_back(hidden_grad)
    layer_grads = [None] * LAYER_COUNT
    gain_rows = [None] * (2 * LAYER_COUNT) + [grad_final_gain]
    for layer_id in reversed(range(LAYER_COUNT)):
        (
            layer_input,
            middle,
            query,
            window_keys,
            window_values,
            log_total,
            attn_out,
            attn_in,
            mlp_in,
            gate_up,
            act_half,
        ) = saved_state[layer_id]
        qkv_full, out_full, gate_up_full, down_full = fetched[layer_id]
        _, mlp_back = jax.vjp(normed, middle, gain_values[2 * layer_id + 1])
        _, act_back = jax.vjp(swiglu, gate_up)
        out_grad = grad_hidden.astype(HALF_TYPE)
        grad_down = contract(act_half, out_grad, 0, 0)
        grad_act = contract(out_grad, down_full, 1, 1)
        grad_gate_up = act_back(grad_act)[0].astype(HALF_TYPE)
        grad_gu_weight = contract(mlp_in, grad_gate_up, 0, 0)
        grad_middle, gain_rows[2 * layer_id + 1] = mlp_back(
            contract(grad_gate_up, gate_up_full, 1, 1)
        )
        grad_hidden = grad_hidden + grad_middle
        branch_grad = grad_hidden.astype(HALF_TYPE)
        grad_out_weight = contract(attn_out, branch_grad, 0, 0)
        grad_attended = contract(branch_grad, out_full, 1, 1).astype(HALF_TYPE)
        query_gradient, window_grad = attend_back(
            query, window_keys, window_values, log_total, grad_attended, position_column
        )
        key_value_gradient = window_grad[back * token_rows :]
        for step in range(1, back + 1):
            part = window_grad[(back - step) * token_rows : (back - step + 1) * token_rows]
            key_value_gradient = key_value_gradient + lax.ppermute(
                part.astype(HALF_TYPE), "ctx", [(i + step, i) for i in range(ctx_count - step)]
            ).astype(WIDE_NUMBER_TYPE)
        _, attn_back = jax.vjp(normed, layer_input, gain_values[2 * layer_id])
        grad_projected = jnp.concatenate(
            [
                rotate_back(
                    query_gradient.reshape(token_rows, QUERY_HEADS, HEAD_SIZE),
                    cosine_table,
                    sine_values,
                ).reshape(token_rows, query_span_width),
                rotate_back(
                    key_value_gradient[:, :key_value_width].reshape(
                        token_rows, KEY_VALUE_HEADS, HEAD_SIZE
                    ),
                    cosine_table,
                    sine_values,
                ).reshape(token_rows, key_value_width),
                key_value_gradient[:, key_value_width:],
            ],
            axis=1,
        ).astype(HALF_TYPE)
        grad_qkv_weight = contract(attn_in, grad_projected, 0, 0)
        grad_input, gain_rows[2 * layer_id] = attn_back(contract(grad_projected, qkv_full, 1, 1))
        grad_hidden = grad_hidden + grad_input
        mlp_grads = lax.psum(
            (exchange_sum(grad_gu_weight, "shard"), exchange_sum(grad_down, "shard")), "ctx"
        )
        attn_grads = lax.psum(
            (exchange_sum(grad_qkv_weight, "shard"), exchange_sum(grad_out_weight, "shard")), "ctx"
        )
        layer_grads[layer_id] = attn_grads + mlp_grads
    every_grad = lax.all_gather(
        grad_hidden.astype(HALF_TYPE), ("ctx", "shard"), axis=0, tiled=True
    )
    own_first = (ctx_index * shard_count + shard_index) * own_rows
    chosen_rows = (own_first + jnp.arange(own_rows))[:, None] == every_id[None, :]
    table_grad = table_grad + contract(chosen_rows.astype(HALF_TYPE), every_grad, 1, 0)
    gain_total = add_all(jnp.stack(gain_rows), ("ctx", "shard"))
    gain_width = norm_gains.shape[1]
    gain_grad = lax.dynamic_slice_in_dim(gain_total, shard_index * gain_width, gain_width, axis=1)
    qkv_grad, out_grad_all, gate_up_grad, down_grad = [
        jnp.stack([layer_grads[layer_no][which] for layer_no in range(LAYER_COUNT)])
        for which in range(4)
    ]
    layer_square = sum(
        (
            jnp.sum(grad_one * grad_one)
            for grad_one in (qkv_grad, out_grad_all, gate_up_grad, down_grad, gain_grad)
        )
    )
    sums = add_all(
        jnp.stack([own_loss, layer_square / ctx_count + jnp.sum(table_grad * table_grad)]),
        ("ctx", "shard"),
    )
    loss_sum, square_sum = sums[0], sums[1]
    grad_norm = jnp.sqrt(square_sum)
    factor = CLIP_NORM / jnp.maximum(grad_norm, CLIP_NORM)
    table_new = advance(embed_table, table_grad, table_mom, table_avg, factor)
    qkv_new = advance(projection_weight, qkv_grad, projection_momentum, projection_average, factor)
    out_new = advance(w_out, out_grad_all, out_mom, out_avg, factor)
    gate_up_new = advance(w_gate_up, gate_up_grad, gate_up_mom, gate_up_avg, factor)
    down_new = advance(w_down, down_grad, down_mom, down_avg, factor)
    gains_new = advance(norm_gains, gain_grad, gain_mom, gain_avg, factor)
    return (
        loss_sum,
        grad_norm,
        table_new[0],
        qkv_new[0],
        out_new[0],
        gate_up_new[0],
        down_new[0],
        gains_new[0],
        table_new[1],
        qkv_new[1],
        out_new[1],
        gate_up_new[1],
        down_new[1],
        gains_new[1],
        table_new[2],
        qkv_new[2],
        out_new[2],
        gate_up_new[2],
        down_new[2],
        gains_new[2],
    )


def solution(mesh):
    return jax.shard_map(
        shards,
        mesh=mesh,
        in_specs=(
            P("shard", "ctx"),
            P("shard", "ctx"),
            P("shard", "ctx"),
            P(("ctx", "shard"), None),
            P(None, "shard", None),
            P(None, "shard", None),
            P(None, "shard", None),
            P(None, "shard", None),
            P(None, "shard"),
            P(("ctx", "shard"), None),
            P(None, "shard", None),
            P(None, "shard", None),
            P(None, "shard", None),
            P(None, "shard", None),
            P(None, "shard"),
            P(("ctx", "shard"), None),
            P(None, "shard", None),
            P(None, "shard", None),
            P(None, "shard", None),
            P(None, "shard", None),
            P(None, "shard"),
        ),
        out_specs=(
            P(),
            P(),
            P(("ctx", "shard"), None),
            P(None, "shard", None),
            P(None, "shard", None),
            P(None, "shard", None),
            P(None, "shard", None),
            P(None, "shard"),
            P(("ctx", "shard"), None),
            P(None, "shard", None),
            P(None, "shard", None),
            P(None, "shard", None),
            P(None, "shard", None),
            P(None, "shard"),
            P(("ctx", "shard"), None),
            P(None, "shard", None),
            P(None, "shard", None),
            P(None, "shard", None),
            P(None, "shard", None),
            P(None, "shard"),
        ),
        check_vma=False,
    )
```

time: 2210 us -> 1280 us (0.58)
  waiting for transfers between devices: 1290 us -> 624 us
  blocking collectives: 259 us -> 67.7 us
  matrix products: 196 us -> 67.5 us
  Pallas kernels: 0 us -> 120 us
  starting transfers between devices: 1.56 us -> 90 us
  loops' own time: 85.2 us -> 0 us
  local copies, waits for them, and re-layouts: 231 us -> 171 us
    reduce_scatter x12 -> x1, waiting for transfers between devices: 541 us -> 101 us  [shards(): lax.psum_scatter(hidden_grad_parts, 'ctx', scatter_dimension=0, tiled=True)]
    unnamed x26 -> x11, waiting for transfers between devices: 369 us -> 1.88 us
    ppermute x0 -> x56, waiting for transfers between devices: none -> 185 us  [the longest x27 123 us: exchange_sum(): lax.ppermute(block(index ^ step).astype(HALF_TYPE), axis, [(i, i ^ step)...]
    all_gather x13 -> x4, blocking collectives: 194 us -> 67.7 us  [the longest x1 43.9 us: shards(): lax.all_gather(jnp.concatenate([token_ids, targets], axis=0), ('ctx', 'sh...]
    pallas_call x0 -> x6, Pallas kernels: none -> 120 us  [the longest x1 56.6 us: vocab_grad(): pl.pallas_call(body, grid=(tokens // tile,), in_specs=[pl.BlockSpec((tile...]
    ppermute x0 -> x56, starting transfers between devices: none -> 85.3 us  [the longest x8 36.2 us: shards(): lax.ppermute(own_kv, 'ctx', [(i, i + step) for i in range(ctx_count - ste...]
    another operation x43 -> x0, loops' own time: 85.2 us -> none  [the longest x2 21 us: attend_forward(): lax.scan(stat_step, start_state, (key_block_list, starts))]
    dot_general x22 -> x17, matrix products: 126 us -> 47.8 us  [contract(): lax.dot_general(left_side, right_side, (((left_dim,), (right_dim,)), ((),...]
  transfers between devices with their start and end apart: 24 -> 68, of which waited for: 17 -> 33; matrix products, arithmetic and copies ran while one was open for 8% -> 13% of each run, Pallas kernels for 0% -> 2%
where the time goes in v1:
time: 1280 us
  waiting for transfers between devices  624 us (49%)
  local copies, waits for them, and re-layouts  171 us (13%)
  Pallas kernels  120 us (9%)
  other arithmetic  112 us (9%)
  starting transfers between devices  90 us (7%)
  blocking collectives  67.7 us (5%)
  matrix products  67.5 us (5%)
  between operations  22.6 us (2%)
    psum x1, waiting for transfers between devices, shards(): lax.psum((exchange_sum(grad_qkv_weight, 'shard'), exchange_sum(grad_out_w...  174 us
    ppermute x27, waiting for transfers between devices, exchange_sum(): lax.ppermute(block(index ^ step).astype(HALF_TYPE), axis, [(i, i ^ step)...  123 us
    reduce_scatter x1, waiting for transfers between devices, shards(): lax.psum_scatter(hidden_grad_parts, 'ctx', scatter_dimension=0, tiled=True)  101 us
    all_gather x1, waiting for transfers between devices, shards(): lax.all_gather(grad_hidden.astype(HALF_TYPE), ('ctx', 'shard'), axis=0, t...  72.7 us
    unnamed x277, local copies, waits for them, and re-layouts  61.2 us
    all_gather x1, waiting for transfers between devices, shards(): sequence_final = lax.all_gather(final_half, 'ctx', axis=0, tiled=True)  60.2 us
    pallas_call x1, Pallas kernels, vocab_grad(): pl.pallas_call(body, grid=(tokens // tile,), in_specs=[pl.BlockSpec((tile...  56.6 us
    dot_general x17, matrix products, contract(): lax.dot_general(left_side, right_side, (((left_dim,), (right_dim,)), ((),...  47.8 us
  transfers between devices with their start and end apart: 68, of which 33 were waited for; matrix products, arithmetic and copies ran while one was open for 13% of the time, Pallas kernels for 2%

profile of v1, /device:TPU:0, one launch (start us, length us, event | category | flops | bytes accessed | tf_op | source)
XLA Modules:
  0.0 1275.5 jit_solution(2833305228463809884)
XLA Ops:
  17.3 43.9 %all-gather.9 = s32[32,2,256]{2,1,0:T(2,128)S(1)} all-gather(s32[1,2,256]{2,1,0:T(2,128)S(1)} %add_bitcast_fusion.8), channel_id=2, replica_groups=mesh['ctx'=8,'shard'=4] {'ctx','shard'}, dimensions={0}, use_global_device_ids=true | all-gather | bytes 67584 | tf_op jit(solution)/shard_map/all_gather | solution.py:335
  62.6 7.7 copy.339
  70.3 11.1 gather_fusion
  87.2 3.7 all-to-all-start
  91.7 5.4 all-gather.11
  97.8 9.5 all-gather.2
  107.3 8.9 all-gather.6
  116.2 29.3 %all-to-all-done = bf16[8,256,576]{1,2,0:T(8,128)(2,1)S(1)} async-done(((bf16[8,256,576]{1,2,0:T(8,128)(2,1)}), bf16[8,256,576]{1,2,0:T(8,128)(2,1)S(1)}, u32[]{:S(2)}, u32[]{:S(2)}) %all-to-all-start) | async-done | bytes 2359328 | tf_op jit(solution)/shard_map/all_to_all | solution.py:347
  154.9 5.8 collective-permute-start.1
  171.1 7.3 attend.2
  179.6 3.4 fusion.10
  192.1 16.5 %collective-permute-start.4 = (bf16[256,384]{1,0:T(8,128)(2,1)S(1)}, bf16[256,384]{1,0:T(8,128)(2,1)}, u32[]{:S(2)}, u32[]{:S(2)}) collective-permute-start(bf16[256,384]{1,0:T(8,128)(2,1)S(1)} %pad_maximum_fusion.11), channel_id=1, source_target_pairs={{0,16},{4,20},{8,24},{12,28},{1,17},{5,21},{9,25},{13,29},{2,18},{... | collective-permute-start | bytes 589832 | tf_op jit(solution)/shard_map/ppermute | solution.py:387
  221.4 7.3 attend.3
  231.3 3.6 fusion.6
  244.9 60.2 %all-gather.22.cloned.1.call-done.final_ref.refs_0_ = bf16[2048,576]{1,0:T(8,128)(2,1)} async-done(((bf16[256,576]{1,0:T(8,128)(2,1)}), bf16[2048,576]{1,0:T(8,128)(2,1)}) %all-gather.22.cloned.1.call-update) | async-done | bytes 2359312 | tf_op jit(solution)/shard_map/all_gather | solution.py:429
  305.2 25.7 %vocab_stats.1 = f32[2048,4]{1,0:T(8,128)} custom-call(bf16[2048,576]{1,0:T(8,128)(2,1)} %all-gather.22.cloned.1.call-done.final_ref.refs_0_, s32[2048,1]{1,0:T(8,128)} %bitcast.237, bf16[4000,576]{1,0:T(8,128)(2,1)} %bitcast.231), custom_call_target="tpu_custom_call" | custom-call | tf_op jit(solution)/shard_map/vocab_stats/pallas_call | solution.py:223
  333.6 3.6 collective-permute-done.8
  345.2 6.9 slice_reduce_fusion
  407.4 5.5 fusion.36.refs_2_
  412.9 56.6 %vocab_grad.1 = (f32[2048,576]{1,0:T(8,128)}, f32[4000,576]{1,0:T(8,128)}) custom-call(bf16[2048,576]{1,0:T(8,128)(2,1)} %all-gather.22.cloned.1.call-done.final_ref.refs_0_, s32[2048,1]{1,0:T(8,128)} %bitcast.238, f32[2048,1]{1,0:T(8,128)} %fusion.36.refs_2_, bf16[4000,576]{1,0:T(8,128)(2,1)} %bitcast.232), custom_call_target="tpu_custom_call" | custom-call | tf_op jit(solution)/shard_map/vocab_grad/pallas_call | solution.py:269
  470.0 101.2 %reduce-scatter.2.cloned.1.call-done = f32[256,576]{1,0:T(8,128)} async-done(((f32[2048,576]{1,0:T(8,128)}), f32[256,576]{1,0:T(8,128)}) %reduce-scatter.2.cloned.1.call-update) | async-done | bytes 589840 | tf_op jit(solution)/shard_map/reduce_scatter | solution.py:459
  580.3 4.2 fusion.62
  594.1 11.5 attend_back.2
  614.3 4.2 dynamic-slice_convert_fusion.5
  630.3 5.1 collective-permute-done.13
  635.3 13.6 %collective-permute-done.14 = bf16[256,384]{1,0:T(8,128)(2,1)S(1)} collective-permute-done((bf16[256,384]{1,0:T(8,128)(2,1)S(1)}, bf16[256,384]{1,0:T(8,128)(2,1)S(1)}, u32[]{:S(2)}, u32[]{:S(2)}) %collective-permute-start.14) | collective-permute-done | bytes 196640 | tf_op jit(solution)/shard_map/ppermute | solution.py:500
  660.2 4.2 fusion.63
  671.2 11.7 attend_back.3
  688.0 4.2 dynamic-slice_convert_fusion.8
  709.1 6.9 collective-permute-done.17
  716.0 9.4 collective-permute-done.18
  730.6 14.4 %collective-permute-done.23 = bf16[144,960]{1,0:T(8,128)(2,1)S(1)} collective-permute-done((bf16[144,960]{1,0:T(8,128)(2,1)}, bf16[144,960]{1,0:T(8,128)(2,1)S(1)}, u32[]{:S(2)}, u32[]{:S(2)}) %collective-permute-start.23) | collective-permute-done | bytes 276512 | tf_op jit(solution)/shard_map/ppermute | solution.py:109
  746.5 3.9 collective-permute-done.24
  757.5 38.7 %collective-permute-done.39 = bf16[384,576]{0,1:T(8,128)(2,1)S(1)} collective-permute-done((bf16[384,576]{0,1:T(8,128)(2,1)S(1)}, bf16[384,576]{0,1:T(8,128)(2,1)S(1)}, u32[]{:S(2)}, u32[]{:S(2)}) %collective-permute-start.39) | collective-permute-done | bytes 442400 | tf_op jit(solution)/shard_map/ppermute | solution.py:109
  800.9 5.2 collective-permute-done.20
  806.1 5.9 collective-permute-done.21
  817.7 16.9 %collective-permute-done.32 = bf16[144,3072]{1,0:T(8,128)(2,1)S(1)} collective-permute-done((bf16[144,3072]{1,0:T(8,128)(2,1)S(1)}, bf16[144,3072]{1,0:T(8,128)(2,1)S(1)}, u32[]{:S(2)}, u32[]{:S(2)}) %collective-permute-start.32) | collective-permute-done | bytes 884768 | tf_op jit(solution)/shard_map/ppermute | solution.py:109
  834.6 17.3 %collective-permute-done.33 = bf16[144,3072]{1,0:T(8,128)(2,1)S(1)} collective-permute-done((bf16[144,3072]{1,0:T(8,128)(2,1)S(1)}, bf16[144,3072]{1,0:T(8,128)(2,1)S(1)}, u32[]{:S(2)}, u32[]{:S(2)}) %collective-permute-start.33) | collective-permute-done | bytes 884768 | tf_op jit(solution)/shard_map/ppermute | solution.py:109
  858.3 4.7 dynamic-slice_convert_fusion.2
  876.9 3.3 copy.411
  903.4 16.6 %collective-permute-done.50 = bf16[1000,576]{0,1:T(8,128)(2,1)} collective-permute-done((bf16[1000,576]{0,1:T(8,128)(2,1)}, bf16[1000,576]{0,1:T(8,128)(2,1)}, u32[]{:S(2)}, u32[]{:S(2)}) %collective-permute-start.50) | collective-permute-done | bytes 1152032 | tf_op jit(solution)/shard_map/ppermute | solution.py:109
  923.2 173.6 %all-reduce.7.cloned.1.call-done = (f32[1,144,960]{2,1,0:T(8,128)}, f32[1,144,960]{2,1,0:T(8,128)}, f32[1,144,576]{2,1,0:T(8,128)}, f32[1,144,576]{2,1,0:T(8,128...) async-done(((f32[1,144,960]{2,1,0:T(8,128)}, f32[1,144,960]{2,1,0:T(8,128)}, f32[1,144,576]{2,1,0:T(8,128)}, ...) | async-done | bytes 7077904 | tf_op jit(solution)/shard_map/psum | solution.py:528
  1112.5 72.7 %all-gather.24.cloned.1.call-done = bf16[8192,576]{1,0:T(8,128)(2,1)} async-done(((bf16[256,576]{1,0:T(8,128)(2,1)}), bf16[8192,576]{1,0:T(8,128)(2,1)}) %all-gather.24.cloned.1.call-update) | async-done | bytes 9437200 | tf_op jit(solution)/shard_map/all_gather | solution.py:532
  1185.2 18.7 %fusion = f32[1000,576]{1,0:T(8,128)} fusion(bf16[8192,576]{1,0:T(8,128)(2,1)} %all-gather.24.cloned.1.call-done, s32[8192]{0:T(1024)} %bitcast.277, s32[1000]{0:T(1024)S(1)} %copy-done.122), kind=kOutput, calls=%fused_computation.1 | convolution fusion | flops 9445376000 | bytes 11777952 | tf_op jit(solution)/shard_map/dot_general | solution.py:75
  1203.9 6.2 multiply_reduce_fusion.1
  1228.7 7.7 add_multiply_fusion.1
  1245.7 5.8 add_multiply_fusion.2
  1251.6 10.0 add_multiply_fusion
  (608 shorter events, 333.2 us)
Async XLA Ops:
  7.2 55.4 %all-gather.38.cloned.1.call-start = ((), (), s32[]{:S(2)}) async-start(), calls=%async_computation.11 | async-start | bytes 5898240 | tf_op jit(solution)/shard_map/all_gather | solution.py:333
  10.1 139.4 %all-gather.26.cloned.1.call-start = ((), (), s32[]{:S(2)}) async-start(), calls=%async_computation.5 | async-start | bytes 1474560 | tf_op jit(solution)/shard_map/all_gather | solution.py:359
  12.6 167.1 %all-gather.28.cloned.1.call-start = ((), (), s32[]{:S(2)}) async-start(), calls=%async_computation.6 | async-start | bytes 4423680 | tf_op jit(solution)/shard_map/all_gather | solution.py:359
  14.2 172.0 %all-gather.30.cloned.1.call-start = ((), (), s32[]{:S(2)}) async-start(), calls=%async_computation.7 | async-start | bytes 2211840 | tf_op jit(solution)/shard_map/all_gather | solution.py:359
  16.1 173.8 %all-gather.32.cloned.1.call-start = ((), (), s32[]{:S(2)}) async-start(), calls=%async_computation.8 | async-start | bytes 1474560 | tf_op jit(solution)/shard_map/all_gather | solution.py:359
  16.7 214.5 %all-gather.34.cloned.1.call-start = ((), (), s32[]{:S(2)}) async-start(), calls=%async_computation.9 | async-start | bytes 4423680 | tf_op jit(solution)/shard_map/all_gather | solution.py:359
  87.2 58.3 %all-to-all-start = ((bf16[8,256,576]{1,2,0:T(8,128)(2,1)}), bf16[8,256,576]{1,2,0:T(8,128)(2,1)S(1)}, u32[]{:S(2)}, u32[]{:S(2)}) async-start(bf16[8,256,576]{1,2,0:T(8,128)(2,1)} %broadcast_select_fusion), calls=%async_computation | async-start | bytes 4718592 | tf_op jit(solution)/shard_map/all_to_all | solution.py:347
  90.9 147.0 %all-gather.36.cloned.1.call-start = ((), (), s32[]{:S(2)}) async-start(), calls=%async_computation.10 | async-start | bytes 2211840 | tf_op jit(solution)/shard_map/all_gather | solution.py:359
  91.7 213.5 %all-gather.22.cloned.1.call-start = ((), (), s32[]{:S(2)}) async-start(), calls=%async_computation.2 | async-start | bytes 2949120 | tf_op jit(solution)/shard_map/all_gather | solution.py:429
  152.7 14.1 %collective-permute-start = (bf16[256,384]{1,0:T(8,128)(2,1)}, bf16[256,384]{1,0:T(8,128)(2,1)}, u32[]{:S(2)}, u32[]{:S(2)}) collective-permute-start(bf16[256,384]{1,0:T(8,128)(2,1)} %pad_maximum_fusion.10), channel_id=1, source_target_pairs={{0,16},{4,20},{8,24},{12,28},{1,17},{5,21},{9,25},{13,29},{2,18},{... | collective-permute-start | bytes 589832 | tf_op jit(solution)/shard_map/ppermute | solution.py:387
  154.9 12.8 %collective-permute-start.1 = (bf16[256,384]{1,0:T(8,128)(2,1)}, bf16[256,384]{1,0:T(8,128)(2,1)}, u32[]{:S(2)}, u32[]{:S(2)}) collective-permute-start(bf16[256,384]{1,0:T(8,128)(2,1)} %pad_maximum_fusion.10), channel_id=1, source_target_pairs={{0,12},{4,16},{8,20},{12,24},{16,28},{1,13},{5,17},{9,21},{13,25},... | collective-permute-start | bytes 589832 | tf_op jit(solution)/shard_map/ppermute | solution.py:387
  192.1 24.8 %collective-permute-start.4 = (bf16[256,384]{1,0:T(8,128)(2,1)S(1)}, bf16[256,384]{1,0:T(8,128)(2,1)}, u32[]{:S(2)}, u32[]{:S(2)}) collective-permute-start(bf16[256,384]{1,0:T(8,128)(2,1)S(1)} %pad_maximum_fusion.11), channel_id=1, source_target_pairs={{0,16},{4,20},{8,24},{12,28},{1,17},{5,21},{9,25},{13,29},{2,18},{... | collective-permute-start | bytes 589832 | tf_op jit(solution)/shard_map/ppermute | solution.py:387
  208.7 9.3 collective-permute-start.5
  210.6 10.2 collective-permute-start.6
  242.7 328.5 %reduce-scatter.2.cloned.1.call-start = ((), (), s32[]{:S(2)}) async-start(), calls=%async_computation.3 | async-start | bytes 5898240 | tf_op jit(solution)/shard_map/reduce_scatter | solution.py:459
  469.5 627.3 %all-reduce.7.cloned.1.call-start = ((), (), s32[]{:S(2)}) async-start(), calls=%async_computation.12 | async-start | bytes 14450688 | tf_op jit(solution)/shard_map/psum | solution.py:528
  611.5 18.7 %collective-permute-start.11 = (bf16[256,384]{1,0:T(8,128)(2,1)S(1)}, bf16[256,384]{1,0:T(8,128)(2,1)S(1)}, u32[]{:S(2)}, u32[]{:S(2)}) collective-permute-start(bf16[256,384]{1,0:T(8,128)(2,1)S(1)} %get-tuple-element.256), channel_id=1, source_target_pairs={{4,0},{8,4},{12,8},{16,12},{20,16},{24,20},{28,24},{5,1},{9,5},{13... | collective-permute-start | bytes 589832 | tf_op jit(solution)/shard_map/ppermute | solution.py:500
  612.8 17.4 %collective-permute-start.12 = (bf16[256,384]{1,0:T(8,128)(2,1)S(1)}, bf16[256,384]{1,0:T(8,128)(2,1)S(1)}, u32[]{:S(2)}, u32[]{:S(2)}) collective-permute-start(bf16[256,384]{1,0:T(8,128)(2,1)S(1)} %get-tuple-element.259), channel_id=1, source_target_pairs={{8,0},{12,4},{16,8},{20,12},{24,16},{28,20},{9,1},{13,5},{17,9},{2... | collective-permute-start | bytes 589832 | tf_op jit(solution)/shard_map/ppermute | solution.py:500
  623.3 12.0 collective-permute-start.13
  626.2 22.7 %collective-permute-start.14 = (bf16[256,384]{1,0:T(8,128)(2,1)S(1)}, bf16[256,384]{1,0:T(8,128)(2,1)S(1)}, u32[]{:S(2)}, u32[]{:S(2)}) collective-permute-start(bf16[256,384]{1,0:T(8,128)(2,1)S(1)} %get-tuple-element.257), channel_id=1, source_target_pairs={{16,0},{20,4},{24,8},{28,12},{17,1},{21,5},{25,9},{29,13},{18,2},{... | collective-permute-start | bytes 589832 | tf_op jit(solution)/shard_map/ppermute | solution.py:500
  629.1 98.4 %collective-permute-start.40 = (bf16[384,576]{0,1:T(8,128)(2,1)}, bf16[384,576]{0,1:T(8,128)(2,1)}, u32[]{:S(2)}, u32[]{:S(2)}) collective-permute-start(bf16[384,576]{0,1:T(8,128)(2,1)} %get-tuple-element.228), channel_id=1, source_target_pairs={{0,1},{1,0},{2,3},{3,2},{4,5},{5,4},{6,7},{7,6},{8,9},{9,8},{10,11... | collective-permute-start | bytes 1327112 | tf_op jit(solution)/shard_map/ppermute | solution.py:109
  686.6 18.3 %collective-permute-start.15 = (bf16[256,384]{1,0:T(8,128)(2,1)S(1)}, bf16[256,384]{1,0:T(8,128)(2,1)S(1)}, u32[]{:S(2)}, u32[]{:S(2)}) collective-permute-start(bf16[256,384]{1,0:T(8,128)(2,1)S(1)} %get-tuple-element.252), channel_id=1, source_target_pairs={{4,0},{8,4},{12,8},{16,12},{20,16},{24,20},{28,24},{5,1},{9,5},{13... | collective-permute-start | bytes 589832 | tf_op jit(solution)/shard_map/ppermute | solution.py:500
  693.9 8.9 collective-permute-start.27
  699.4 9.0 collective-permute-start.16
  700.7 15.3 %collective-permute-start.17 = (bf16[256,384]{1,0:T(8,128)(2,1)S(1)}, bf16[256,384]{1,0:T(8,128)(2,1)S(1)}, u32[]{:S(2)}, u32[]{:S(2)}) collective-permute-start(bf16[256,384]{1,0:T(8,128)(2,1)S(1)} %get-tuple-element.254), channel_id=1, source_target_pairs={{12,0},{16,4},{20,8},{24,12},{28,16},{13,1},{17,5},{21,9},{25,13},... | collective-permute-start | bytes 589832 | tf_op jit(solution)/shard_map/ppermute | solution.py:500
  702.8 22.6 %collective-permute-start.18 = (bf16[256,384]{1,0:T(8,128)(2,1)S(1)}, bf16[256,384]{1,0:T(8,128)(2,1)S(1)}, u32[]{:S(2)}, u32[]{:S(2)}) collective-permute-start(bf16[256,384]{1,0:T(8,128)(2,1)S(1)} %get-tuple-element.253), channel_id=1, source_target_pairs={{16,0},{20,4},{24,8},{28,12},{17,1},{21,5},{25,9},{29,13},{18,2},{... | collective-permute-start | bytes 589832 | tf_op jit(solution)/shard_map/ppermute | solution.py:500
  704.9 22.6 %collective-permute-start.41 = (bf16[384,576]{0,1:T(8,128)(2,1)}, bf16[384,576]{0,1:T(8,128)(2,1)}, u32[]{:S(2)}, u32[]{:S(2)}) collective-permute-start(bf16[384,576]{0,1:T(8,128)(2,1)} %get-tuple-element.230), channel_id=1, source_target_pairs={{0,2},{1,3},{2,0},{3,1},{4,6},{5,7},{6,4},{7,5},{8,10},{9,11},{10,... | collective-permute-start | bytes 1327112 | tf_op jit(solution)/shard_map/ppermute | solution.py:109
  708.4 19.7 %collective-permute-start.42 = (bf16[384,576]{0,1:T(8,128)(2,1)}, bf16[384,576]{0,1:T(8,128)(2,1)}, u32[]{:S(2)}, u32[]{:S(2)}) collective-permute-start(bf16[384,576]{0,1:T(8,128)(2,1)} %get-tuple-element.229), channel_id=1, source_target_pairs={{0,3},{1,2},{2,1},{3,0},{4,7},{5,6},{6,5},{7,4},{8,11},{9,10},{10,... | collective-permute-start | bytes 1327112 | tf_op jit(solution)/shard_map/ppermute | solution.py:109
  716.0 36.2 %collective-permute-start.37 = (bf16[384,576]{0,1:T(8,128)(2,1)}, bf16[384,576]{0,1:T(8,128)(2,1)}, u32[]{:S(2)}, u32[]{:S(2)}) collective-permute-start(bf16[384,576]{0,1:T(8,128)(2,1)} %get-tuple-element.231), channel_id=1, source_target_pairs={{0,1},{1,0},{2,3},{3,2},{4,5},{5,4},{6,7},{7,6},{8,9},{9,8},{10,11... | collective-permute-start | bytes 1327112 | tf_op jit(solution)/shard_map/ppermute | solution.py:109
  725.4 26.9 %collective-permute-start.38 = (bf16[384,576]{0,1:T(8,128)(2,1)}, bf16[384,576]{0,1:T(8,128)(2,1)}, u32[]{:S(2)}, u32[]{:S(2)}) collective-permute-start(bf16[384,576]{0,1:T(8,128)(2,1)} %get-tuple-element.233), channel_id=1, source_target_pairs={{0,2},{1,3},{2,0},{3,1},{4,6},{5,7},{6,4},{7,5},{8,10},{9,11},{10,... | collective-permute-start | bytes 1327112 | tf_op jit(solution)/shard_map/ppermute | solution.py:109
  727.6 17.4 %collective-permute-start.23 = (bf16[144,960]{1,0:T(8,128)(2,1)}, bf16[144,960]{1,0:T(8,128)(2,1)S(1)}, u32[]{:S(2)}, u32[]{:S(2)}) collective-permute-start(bf16[144,960]{1,0:T(8,128)(2,1)} %get-tuple-element.236), channel_id=1, source_target_pairs={{0,2},{1,3},{2,0},{3,1},{4,6},{5,7},{6,4},{7,5},{8,10},{9,11},{10,... | collective-permute-start | bytes 829448 | tf_op jit(solution)/shard_map/ppermute | solution.py:109
  728.1 22.3 %collective-permute-start.24 = (bf16[144,960]{1,0:T(8,128)(2,1)}, bf16[144,960]{1,0:T(8,128)(2,1)S(1)}, u32[]{:S(2)}, u32[]{:S(2)}) collective-permute-start(bf16[144,960]{1,0:T(8,128)(2,1)} %get-tuple-element.235), channel_id=1, source_target_pairs={{0,3},{1,2},{2,1},{3,0},{4,7},{5,6},{6,5},{7,4},{8,11},{9,10},{10,... | collective-permute-start | bytes 829448 | tf_op jit(solution)/shard_map/ppermute | solution.py:109
  730.0 83.5 %collective-permute-start.34 = (bf16[144,3072]{1,0:T(8,128)(2,1)S(1)}, bf16[144,3072]{1,0:T(8,128)(2,1)S(1)}, u32[]{:S(2)}, u32[]{:S(2)}) collective-permute-start(bf16[144,3072]{1,0:T(8,128)(2,1)S(1)} %copy-done.73), channel_id=1, source_target_pairs={{0,1},{1,0},{2,3},{3,2},{4,5},{5,4},{6,7},{7,6},{8,9},{9,8},{10,11... | collective-permute-start | bytes 2654216 | tf_op jit(solution)/shard_map/ppermute | solution.py:109
  744.9 69.6 %collective-permute-start.35 = (bf16[144,3072]{1,0:T(8,128)(2,1)S(1)}, bf16[144,3072]{1,0:T(8,128)(2,1)S(1)}, u32[]{:S(2)}, u32[]{:S(2)}) collective-permute-start(bf16[144,3072]{1,0:T(8,128)(2,1)S(1)} %copy-done.72), channel_id=1, source_target_pairs={{0,2},{1,3},{2,0},{3,1},{4,6},{5,7},{6,4},{7,5},{8,10},{9,11},{10,... | collective-permute-start | bytes 2654216 | tf_op jit(solution)/shard_map/ppermute | solution.py:109
  750.4 64.1 %collective-permute-start.36 = (bf16[144,3072]{1,0:T(8,128)(2,1)S(1)}, bf16[144,3072]{1,0:T(8,128)(2,1)S(1)}, u32[]{:S(2)}, u32[]{:S(2)}) collective-permute-start(bf16[144,3072]{1,0:T(8,128)(2,1)S(1)} %copy-done.71), channel_id=1, source_target_pairs={{0,3},{1,2},{2,1},{3,0},{4,7},{5,6},{6,5},{7,4},{8,11},{9,10},{10,... | collective-permute-start | bytes 2654216 | tf_op jit(solution)/shard_map/ppermute | solution.py:109
  752.2 44.0 %collective-permute-start.39 = (bf16[384,576]{0,1:T(8,128)(2,1)S(1)}, bf16[384,576]{0,1:T(8,128)(2,1)S(1)}, u32[]{:S(2)}, u32[]{:S(2)}) collective-permute-start(bf16[384,576]{0,1:T(8,128)(2,1)S(1)} %copy-done.81), channel_id=1, source_target_pairs={{0,3},{1,2},{2,1},{3,0},{4,7},{5,6},{6,5},{7,4},{8,11},{9,10},{10,... | collective-permute-start | bytes 1327112 | tf_op jit(solution)/shard_map/ppermute | solution.py:109
  752.3 45.0 %collective-permute-start.19 = (bf16[144,960]{1,0:T(8,128)(2,1)S(1)}, bf16[144,960]{1,0:T(8,128)(2,1)S(1)}, u32[]{:S(2)}, u32[]{:S(2)}) collective-permute-start(bf16[144,960]{1,0:T(8,128)(2,1)S(1)} %get-tuple-element.237), channel_id=1, source_target_pairs={{0,1},{1,0},{2,3},{3,2},{4,5},{5,4},{6,7},{7,6},{8,9},{9,8},{10,11... | collective-permute-start | bytes 829448 | tf_op jit(solution)/shard_map/ppermute | solution.py:109
  796.2 9.9 collective-permute-start.20
  797.3 14.8 %collective-permute-start.21 = (bf16[144,960]{1,0:T(8,128)(2,1)S(1)}, bf16[144,960]{1,0:T(8,128)(2,1)S(1)}, u32[]{:S(2)}, u32[]{:S(2)}) collective-permute-start(bf16[144,960]{1,0:T(8,128)(2,1)S(1)} %get-tuple-element.238), channel_id=1, source_target_pairs={{0,3},{1,2},{2,1},{3,0},{4,7},{5,6},{6,5},{7,4},{8,11},{9,10},{10,... | collective-permute-start | bytes 829448 | tf_op jit(solution)/shard_map/ppermute | solution.py:109
  806.1 11.6 collective-permute-start.31
  812.1 22.5 %collective-permute-start.32 = (bf16[144,3072]{1,0:T(8,128)(2,1)S(1)}, bf16[144,3072]{1,0:T(8,128)(2,1)S(1)}, u32[]{:S(2)}, u32[]{:S(2)}) collective-permute-start(bf16[144,3072]{1,0:T(8,128)(2,1)S(1)} %copy-done.75), channel_id=1, source_target_pairs={{0,2},{1,3},{2,0},{3,1},{4,6},{5,7},{6,4},{7,5},{8,10},{9,11},{10,... | collective-permute-start | bytes 2654216 | tf_op jit(solution)/shard_map/ppermute | solution.py:109
  813.5 38.4 %collective-permute-start.33 = (bf16[144,3072]{1,0:T(8,128)(2,1)S(1)}, bf16[144,3072]{1,0:T(8,128)(2,1)S(1)}, u32[]{:S(2)}, u32[]{:S(2)}) collective-permute-start(bf16[144,3072]{1,0:T(8,128)(2,1)S(1)} %copy-done.74), channel_id=1, source_target_pairs={{0,3},{1,2},{2,1},{3,0},{4,7},{5,6},{6,5},{7,4},{8,11},{9,10},{10,... | collective-permute-start | bytes 2654216 | tf_op jit(solution)/shard_map/ppermute | solution.py:109
  855.1 330.1 %all-gather.24.cloned.1.call-start = ((), (), s32[]{:S(2)}) async-start(), calls=%async_computation.4 | async-start | bytes 10813440 | tf_op jit(solution)/shard_map/all_gather | solution.py:532
  864.9 33.3 %collective-permute-start.48 = (bf16[1000,576]{0,1:T(8,128)(2,1)}, bf16[1000,576]{0,1:T(8,128)(2,1)}, u32[]{:S(2)}, u32[]{:S(2)}) collective-permute-start(bf16[1000,576]{0,1:T(8,128)(2,1)} %copy.401), channel_id=1, source_target_pairs={{0,1},{1,0},{2,3},{3,2},{4,5},{5,4},{6,7},{7,6},{8,9},{9,8},{10,11... | collective-permute-start | bytes 3456008 | tf_op jit(solution)/shard_map/ppermute | solution.py:109
  867.4 33.5 %collective-permute-start.49 = (bf16[1000,576]{0,1:T(8,128)(2,1)}, bf16[1000,576]{0,1:T(8,128)(2,1)}, u32[]{:S(2)}, u32[]{:S(2)}) collective-permute-start(bf16[1000,576]{0,1:T(8,128)(2,1)} %copy.403), channel_id=1, source_target_pairs={{0,2},{1,3},{2,0},{3,1},{4,6},{5,7},{6,4},{7,5},{8,10},{9,11},{10,... | collective-permute-start | bytes 3456008 | tf_op jit(solution)/shard_map/ppermute | solution.py:109
  871.0 49.0 %collective-permute-start.50 = (bf16[1000,576]{0,1:T(8,128)(2,1)}, bf16[1000,576]{0,1:T(8,128)(2,1)}, u32[]{:S(2)}, u32[]{:S(2)}) collective-permute-start(bf16[1000,576]{0,1:T(8,128)(2,1)} %copy.405), channel_id=1, source_target_pairs={{0,3},{1,2},{2,1},{3,0},{4,7},{5,6},{6,5},{7,4},{8,11},{9,10},{10,... | collective-permute-start | bytes 3456008 | tf_op jit(solution)/shard_map/ppermute | solution.py:109
  871.4 10.9 collective-permute-start.43
  895.4 27.2 %collective-permute-start.47 = (f32[5,576]{1,0:T(8,128)S(1)}, f32[5,576]{1,0:T(8,128)S(1)}, u32[]{:S(2)}, u32[]{:S(2)}) collective-permute-start(f32[5,576]{1,0:T(8,128)S(1)} %add.619), channel_id=1, source_target_pairs={{0,2},{1,3},{2,0},{3,1},{4,6},{5,7},{6,4},{7,5},{8,10},{9,11},{10,... | collective-permute-start | bytes 34568 | tf_op jit(solution)/shard_map/ppermute | solution.py:87
  (146 other events, 1366.7 us)
Sparse Core Ops, SparseCore 0:
  10.2 40.6 all-gather.37
  53.1 17.4 all-gather.25
  72.7 31.4 all-gather.27
  106.2 20.3 all-gather.29
  128.6 17.4 all-gather.31
  148.0 30.7 all-gather.33
  180.9 20.6 all-gather.35
  242.8 62.3 all-gather.21
  469.7 101.4 reduce-scatter.1
  855.2 241.6 all-reduce.6
  1100.3 84.7 all-gather.23

commit v2 on v1

--- a/solution.py
+++ b/solution.py
@@ -99,15 +99,20 @@
 def exchange_sum(partial, axis):
     count = lax.axis_size(axis)
     index = lax.axis_index(axis)
+    core = index % 2
+    place = index // 2
     rows = partial.shape[0] // count
-
-    def block(which):
-        return lax.dynamic_slice_in_dim(partial, which * rows, rows, axis=0)
-
-    total = block(index)
-    for step in range(1, count):
+    blocks = partial.reshape(count // 2, 2, rows, partial.shape[1])
+    half = lax.dynamic_index_in_dim(blocks, core, axis=1, keepdims=False) + lax.ppermute(
+        lax.dynamic_index_in_dim(blocks, 1 - core, axis=1, keepdims=False),
+        axis,
+        [(i, i ^ 1) for i in range(count)],
+    )
+    total = lax.dynamic_index_in_dim(half, place, axis=0, keepdims=False)
+    for step in range(1, count // 2):
+        leaving = lax.dynamic_index_in_dim(half, place ^ step, axis=0, keepdims=False)
         sent = lax.ppermute(
-            block(index ^ step).astype(HALF_TYPE), axis, [(i, i ^ step) for i in range(count)]
+            leaving.astype(HALF_TYPE), axis, [(i, i ^ (2 * step)) for i in range(count)]
         )
         total = total + sent.astype(WIDE_NUMBER_TYPE)
     return total
@@ -208,12 +213,31 @@
     logit_sum = jnp.sum(logits, axis=1, keepdims=True)
     column = lax.broadcasted_iota(jnp.int32, logits.shape, 1)
     chosen = jnp.sum(jnp.where(column == target_ref[...], logits, 0.0), axis=1, keepdims=True)
-    out_ref[:, 0:1] = row_max
-    out_ref[:, 1:2] = exp_sum
-    out_ref[:, 2:3] = logit_sum
-    out_ref[:, 3:4] = chosen
-
-
+    rows = logits.shape[0]
+    columns = jnp.concatenate(
+        [row_max, exp_sum, logit_sum, chosen, jnp.zeros((rows, 124), WIDE_NUMBER_TYPE)], axis=1
+    )
+    out_ref[...] = columns.T[:STAT_ROWS]
+
+
+def combine_kernel(first_ref, second_ref, out_ref):
+    joint_max = jnp.maximum(first_ref[0:1], second_ref[0:1])
+    out_ref[...] = first_ref[...] + second_ref[...]
+    out_ref[0:1] = joint_max
+    out_ref[1:2] = first_ref[1:2] * jnp.exp(first_ref[0:1] - joint_max) + second_ref[
+        1:2
+    ] * jnp.exp(second_ref[0:1] - joint_max)
+
+
+def combine_stats(first, second):
+    return pl.pallas_call(
+        combine_kernel,
+        out_shape=jax.ShapeDtypeStruct(first.shape, WIDE_NUMBER_TYPE),
+        name="combine_stats",
+    )(first, second)
+
+
+STAT_ROWS = 8
 TOKEN_TILE = 256
 
 
@@ -228,18 +252,19 @@
             pl.BlockSpec((tile, 1), lambda i: (i, 0)),
             pl.BlockSpec(table_rows.shape, lambda i: (0, 0), pipeline_mode=pl.Buffered(1)),
         ],
-        out_specs=pl.BlockSpec((tile, 4), lambda i: (i, 0)),
-        out_shape=jax.ShapeDtypeStruct((tokens, 4), WIDE_NUMBER_TYPE),
+        out_specs=pl.BlockSpec((STAT_ROWS, tile), lambda i: (0, i)),
+        out_shape=jax.ShapeDtypeStruct((STAT_ROWS, tokens), WIDE_NUMBER_TYPE),
         compiler_params=pltpu.CompilerParams(vmem_limit_bytes=56 << 20),
         name="vocab_stats",
     )(finals, target_column, table_rows)
 
 
-def vocab_grad_kernel(all_tokens, final_ref, target_ref, lse_ref, table_ref, dx_ref, dw_ref):
+def vocab_grad_kernel(all_tokens, final_ref, target_ref, stat_ref, table_ref, dx_ref, dw_ref):
     finals = final_ref[...]
     table = table_ref[...]
     logits = contract(finals, table, 1, 1)
-    lse = lse_ref[...]
+    lse_row = stat_ref[0:1] + jnp.log(stat_ref[1:2])
+    lse = jnp.broadcast_to(lse_row, (128, lse_row.shape[1])).T[:, 0:1]
     column = lax.broadcasted_iota(jnp.int32, logits.shape, 1)
     grad = (
         jnp.exp(logits - lse) * (1.0 + 2.0 * Z_WEIGHT * lse)
@@ -247,7 +272,7 @@
         - SMOOTH / V
     ) / all_tokens
     grad = grad.astype(HALF_TYPE)
-    dx_ref[...] = contract(grad, table, 1, 0)
+    dx_ref[...] = contract(grad, table, 1, 0).astype(HALF_TYPE)
     part = contract(grad, finals, 0, 0)
 
     @pl.when(pl.program_id(0) == 0)
@@ -259,7 +284,7 @@
         dw_ref[...] += part
 
 
-def vocab_grad(finals, target_column, lse_column, table_rows, all_tokens):
+def vocab_grad(finals, target_column, stats, table_rows, all_tokens):
     tokens = finals.shape[0]
     tile = TOKEN_TILE
 
@@ -272,7 +297,7 @@
         in_specs=[
             pl.BlockSpec((tile, MODEL_WIDTH), lambda i: (i, 0)),
             pl.BlockSpec((tile, 1), lambda i: (i, 0)),
-            pl.BlockSpec((tile, 1), lambda i: (i, 0)),
+            pl.BlockSpec((STAT_ROWS, tile), lambda i: (0, i)),
             pl.BlockSpec(table_rows.shape, lambda i: (0, 0), pipeline_mode=pl.Buffered(1)),
         ],
         out_specs=(
@@ -280,12 +305,12 @@
             pl.BlockSpec(table_rows.shape, lambda i: (0, 0), pipeline_mode=pl.Buffered(1)),
         ),
         out_shape=(
-            jax.ShapeDtypeStruct((tokens, MODEL_WIDTH), WIDE_NUMBER_TYPE),
+            jax.ShapeDtypeStruct((tokens, MODEL_WIDTH), HALF_TYPE),
             jax.ShapeDtypeStruct(table_rows.shape, WIDE_NUMBER_TYPE),
         ),
         compiler_params=pltpu.CompilerParams(vmem_limit_bytes=60 << 20),
         name="vocab_grad",
-    )(finals, target_column, lse_column, table_rows)
+    )(finals, target_column, stats, table_rows)
 
 
 def advance(weight, grad_one, moment, average, factor):
@@ -335,7 +360,6 @@
     pairs = lax.all_gather(
         jnp.concatenate([token_ids, targets], axis=0), ("ctx", "shard"), axis=0
     ).reshape(ctx_count, shard_count, 2, token_rows)
-    every_id = pairs[:, :, 0].reshape(all_tokens)
     sequence_pairs = lax.dynamic_index_in_dim(pairs, shard_index, axis=1, keepdims=False)
     first_row = ctx_index * slice_rows
     id_row = sequence_pairs[:, 0].reshape(sequence) - first_row
@@ -428,20 +452,11 @@
     final_half = normed(hidden, final_gain).astype(HALF_TYPE)
     sequence_final = lax.all_gather(final_half, "ctx", axis=0, tiled=True)
 
-    def combine(first_stats, second_stats):
-        joint_max = jnp.maximum(first_stats[0], second_stats[0])
-        return jnp.stack(
-            [
-                joint_max,
-                first_stats[1] * jnp.exp(first_stats[0] - joint_max)
-                + second_stats[1] * jnp.exp(second_stats[0] - joint_max),
-                first_stats[2] + second_stats[2],
-                first_stats[3] + second_stats[3],
-            ]
-        )
-
-    stats = vocab_stats(sequence_final, target_column, table_rows).T
-    stats = butterfly(stats, "ctx", combine)
+    stats = vocab_stats(sequence_final, target_column, table_rows)
+    stats = butterfly(stats, "ctx", combine_stats)
+    hidden_grad_parts, slice_grad = vocab_grad(
+        sequence_final, target_column, stats, table_rows, all_tokens
+    )
     row_lse = stats[0] + jnp.log(stats[1])
     token_loss = (
         row_lse
@@ -453,11 +468,12 @@
         jnp.sum(lax.dynamic_slice_in_dim(token_loss, ctx_index * token_rows, token_rows))
         / all_tokens
     )
-    hidden_grad_parts, slice_grad = vocab_grad(
-        sequence_final, target_column, row_lse[:, None], table_rows, all_tokens
-    )
-    hidden_grad = lax.psum_scatter(hidden_grad_parts, "ctx", scatter_dimension=0, tiled=True)
-    table_grad = exchange_sum(slice_grad, "shard")
+    hidden_grad = jnp.sum(
+        lax.all_to_all(
+            hidden_grad_parts.reshape(ctx_count, token_rows, MODEL_WIDTH), "ctx", 0, 0, tiled=True
+        ).astype(WIDE_NUMBER_TYPE),
+        axis=0,
+    )
     _, final_back = jax.vjp(normed, hidden, final_gain)
     grad_hidden, grad_final_gain = final_back(hidden_grad)
     layer_grads = [None] * LAYER_COUNT
@@ -491,6 +507,13 @@
         branch_grad = grad_hidden.astype(HALF_TYPE)
         grad_out_weight = contract(attn_out, branch_grad, 0, 0)
         grad_attended = contract(branch_grad, out_full, 1, 1).astype(HALF_TYPE)
+        if layer_id < LAYER_COUNT - 1:
+            above = layer_grads[layer_id + 1]
+            grad_attended, above_mlp = lax.optimization_barrier((grad_attended, above[2:]))
+            layer_grads[layer_id + 1] = above[:2] + above_mlp
+        mlp_grads = tuple(
+            exchange_sum(partial, "shard") for partial in (grad_gu_weight, grad_down)
+        )
         query_gradient, window_grad = attend_back(
             query, window_keys, window_values, log_total, grad_attended, position_column
         )
@@ -522,19 +545,21 @@
         grad_qkv_weight = contract(attn_in, grad_projected, 0, 0)
         grad_input, gain_rows[2 * layer_id] = attn_back(contract(grad_projected, qkv_full, 1, 1))
         grad_hidden = grad_hidden + grad_input
-        mlp_grads = lax.psum(
-            (exchange_sum(grad_gu_weight, "shard"), exchange_sum(grad_down, "shard")), "ctx"
-        )
-        attn_grads = lax.psum(
-            (exchange_sum(grad_qkv_weight, "shard"), exchange_sum(grad_out_weight, "shard")), "ctx"
+        attn_grads = tuple(
+            exchange_sum(partial, "shard") for partial in (grad_qkv_weight, grad_out_weight)
         )
         layer_grads[layer_id] = attn_grads + mlp_grads
-    every_grad = lax.all_gather(
-        grad_hidden.astype(HALF_TYPE), ("ctx", "shard"), axis=0, tiled=True
-    )
-    own_first = (ctx_index * shard_count + shard_index) * own_rows
-    chosen_rows = (own_first + jnp.arange(own_rows))[:, None] == every_id[None, :]
-    table_grad = table_grad + contract(chosen_rows.astype(HALF_TYPE), every_grad, 1, 0)
+    sequence_grad = lax.all_gather(grad_hidden.astype(HALF_TYPE), "ctx", axis=0, tiled=True)
+    last = LAYER_COUNT - 1
+    early = lax.psum(layer_grads[last][2:], "ctx")
+    late = tuple(layer_grads[:last]) + (layer_grads[last][:2],)
+    early, late = lax.optimization_barrier((early, late))
+    late = lax.psum(late, "ctx")
+    layer_grads = list(late[:last]) + [late[last] + early]
+    chosen_rows = jnp.arange(slice_rows)[:, None] == id_row[None, :]
+    table_grad = exchange_sum(
+        slice_grad + contract(chosen_rows.astype(HALF_TYPE), sequence_grad, 1, 0), "shard"
+    )
     gain_total = add_all(jnp.stack(gain_rows), ("ctx", "shard"))
     gain_width = norm_gains.shape[1]
     gain_grad = lax.dynamic_slice_in_dim(gain_total, shard_index * gain_width, gain_width, axis=1)

time: 1280 us -> 1080 us (0.84)
  waiting for transfers between devices: 624 us -> 446 us
  local copies, waits for them, and re-layouts: 171 us -> 143 us
    reduce_scatter x1 -> x0, waiting for transfers between devices: 101 us -> none  [shards(): lax.psum_scatter(hidden_grad_parts, 'ctx', scatter_dimension=0, tiled=True)]
    ppermute x27 -> x18, waiting for transfers between devices: 123 us -> 33.1 us  [the longest x9 33.1 us: exchange_sum(): lax.ppermute(leaving.astype(HALF_TYPE), axis, [(i, i ^ 2 * step) for i in...]
    all_to_all x0 -> x1, waiting for transfers between devices: none -> 47.6 us  [shards(): lax.all_to_all(hidden_grad_parts.reshape(ctx_count, token_rows, MODEL_WID...]
    all_gather x1, waiting for transfers between devices: 72.7 us -> 28.4 us  [shards(): lax.all_gather(grad_hidden.astype(HALF_TYPE), 'ctx', axis=0, tiled=True)]
    add x4 -> x18, other arithmetic: 6.65 us -> 42 us  [the longest x9 18.3 us: exchange_sum(): lax.dynamic_index_in_dim(blocks, core, axis=1, keepdims=False)]
    dynamic_slice x0 -> x7, local copies, waits for them, and re-layouts: none -> 32.9 us  [the longest x4 25.7 us: exchange_sum(): lax.dynamic_index_in_dim(blocks, core, axis=1, keepdims=False)]
    convert_element_type x13 -> x9, local copies, waits for them, and re-layouts: 30.3 us -> 4.32 us  [exchange_sum(): leaving.astype(HALF_TYPE)]
    psum x1 -> x2, waiting for transfers between devices: 174 us -> 198 us  [the longest x1 139 us: shards(): late = lax.psum(late, 'ctx')]
  transfers between devices with their start and end apart: 68 -> 60, of which waited for: 33 -> 27; matrix products, arithmetic and copies ran while one was open for 13% -> 22% of each run, Pallas kernels for 2% -> 2%
where the time goes in v2:
time: 1080 us; the launch traced here: 1070 us
  waiting for transfers between devices  446 us (41%)
  local copies, waits for them, and re-layouts  143 us (13%)
  Pallas kernels  124 us (11%)
  other arithmetic  115 us (11%)
  starting transfers between devices  81.4 us (8%)
  matrix products  69 us (6%)
  blocking collectives  68 us (6%)
  between operations  22.6 us (2%)
    psum x1, waiting for transfers between devices, shards(): late = lax.psum(late, 'ctx')  139 us
    psum x1, waiting for transfers between devices, shards(): early = lax.psum(layer_grads[last][2:], 'ctx')  59.3 us
    all_gather x1, waiting for transfers between devices, shards(): sequence_final = lax.all_gather(final_half, 'ctx', axis=0, tiled=True)  57.9 us
    pallas_call x1, Pallas kernels, vocab_grad(): pl.pallas_call(body, grid=(tokens // tile,), in_specs=[pl.BlockSpec((tile...  56.5 us
    dot_general x17, matrix products, contract(): lax.dot_general(left_side, right_side, (((left_dim,), (right_dim,)), ((),...  48.3 us
    all_to_all x1, waiting for transfers between devices, shards(): lax.all_to_all(hidden_grad_parts.reshape(ctx_count, token_rows, MODEL_WID...  47.6 us
    all_gather x1, blocking collectives, shards(): lax.all_gather(jnp.concatenate([token_ids, targets], axis=0), ('ctx', 'sh...  43.9 us
    unnamed x246, local copies, waits for them, and re-layouts  38.1 us
  transfers between devices with their start and end apart: 60, of which 27 were waited for; matrix products, arithmetic and copies ran while one was open for 22% of the time, Pallas kernels for 2%

profile of v2, /device:TPU:0, one launch (start us, length us, event | category | flops | bytes accessed | tf_op | source)
XLA Modules:
  0.0 1069.0 jit_solution(4712842215959295876)
XLA Ops:
  17.3 43.9 %all-gather.9 = s32[32,2,256]{2,1,0:T(2,128)S(1)} all-gather(s32[1,2,256]{2,1,0:T(2,128)S(1)} %add_bitcast_fusion), channel_id=2, replica_groups=mesh['ctx'=8,'shard'=4] {'ctx','shard'}, dimensions={0}, use_global_device_ids=true | all-gather | bytes 67584 | tf_op jit(solution)/shard_map/all_gather | solution.py:360
  62.0 7.7 copy.211
  69.7 11.1 %gather_fusion = bf16[2048,576]{1,0:T(8,128)(2,1)S(1)} fusion(bf16[4000,576]{1,0:T(8,128)(2,1)} %bitcast.235, s32[2048]{0:T(1024)S(1)} %broadcast_clamp_fusion), kind=kCustom, calls=%fused_computation | custom fusion | bytes 4726784 | tf_op jit(solution)/shard_map/gather | solution.py:369
  86.5 3.7 all-to-all-start
  91.9 5.4 all-gather.11
  99.4 8.9 all-gather.2
  108.3 9.8 all-gather.6
  118.1 26.7 %all-to-all-done = bf16[8,256,576]{1,2,0:T(8,128)(2,1)S(1)} async-done(((bf16[8,256,576]{1,2,0:T(8,128)(2,1)}), bf16[8,256,576]{1,2,0:T(8,128)(2,1)S(1)}, u32[]{:S(2)}, u32[]{:S(2)}) %all-to-all-start) | async-done | bytes 2359328 | tf_op jit(solution)/shard_map/all_to_all | solution.py:371
  154.9 5.8 collective-permute-start.1
  168.9 7.3 attend.2
  192.9 17.6 %collective-permute-start.4 = (bf16[256,384]{1,0:T(8,128)(2,1)S(1)}, bf16[256,384]{1,0:T(8,128)(2,1)}, u32[]{:S(2)}, u32[]{:S(2)}) collective-permute-start(bf16[256,384]{1,0:T(8,128)(2,1)S(1)} %pad_maximum_fusion.13), channel_id=1, source_target_pairs={{0,16},{4,20},{8,24},{12,28},{1,17},{5,21},{9,25},{13,29},{2,18},{... | collective-permute-start | bytes 589832 | tf_op jit(solution)/shard_map/ppermute | solution.py:411
  224.1 7.3 attend.3
  234.6 3.7 fusion.4
  249.4 57.9 %all-gather.22.cloned.1.call-done.final_ref.refs_0_ = bf16[2048,576]{1,0:T(8,128)(2,1)} async-done(((bf16[256,576]{1,0:T(8,128)(2,1)}), bf16[2048,576]{1,0:T(8,128)(2,1)}) %all-gather.22.cloned.1.call-update) | async-done | bytes 2359312 | tf_op jit(solution)/shard_map/all_gather | solution.py:453
  307.4 26.0 %vocab_stats.1.first_ref = f32[8,2048]{1,0:T(8,128)} custom-call(bf16[2048,576]{1,0:T(8,128)(2,1)} %all-gather.22.cloned.1.call-done.final_ref.refs_0_, s32[2048,1]{1,0:T(8,128)} %bitcast.250, bf16[4000,576]{1,0:T(8,128)(2,1)} %bitcast.236), custom_call_target="tpu_custom_call" | custom-call | tf_op jit(solution)/shard_map/vocab_stats/pallas_call | solution.py:247
  333.9 4.0 collective-permute-done.8.second_ref
  347.5 3.6 collective-permute-done.10.second_ref
  352.5 56.5 %vocab_grad.1 = (bf16[2048,576]{1,0:T(8,128)(2,1)}, f32[4000,576]{1,0:T(8,128)}) custom-call(bf16[2048,576]{1,0:T(8,128)(2,1)} %all-gather.22.cloned.1.call-done.final_ref.refs_0_, s32[2048,1]{1,0:T(8,128)} %bitcast.251, f32[8,2048]{1,0:T(8,128)} %combine_stats.5.refs_2_, bf16[4000,576]{1,0:T(8,128)(2,1)} %bitcast.237), custom_call_target="tpu_custom_call" | custom-call | tf_op jit(solution)/shard_map/vocab_grad/pallas_call | solution.py:294
  409.1 4.3 copy.230
  413.4 4.4 all-to-all-start.1
  419.6 47.6 %all-to-all-done.1 = bf16[8,256,576]{1,2,0:T(8,128)(2,1)} async-done(((bf16[8,256,576]{1,2,0:T(8,128)(2,1)}), bf16[8,256,576]{1,2,0:T(8,128)(2,1)}, u32[]{:S(2)}, u32[]{:S(2)}) %all-to-all-start.1) | async-done | bytes 2359328 | tf_op jit(solution)/shard_map/all_to_all | solution.py:472
  481.4 4.0 fusion.54
  495.0 11.5 %attend_back.2 = (f32[256,576]{1,0:T(8,128)S(1)}, f32[1280,384]{1,0:T(8,128)S(1)}) custom-call(bf16[256,576]{1,0:T(8,128)(2,1)S(1)} %copy.224.query_ref, bf16[1280,192]{1,0:T(8,128)(2,1)S(1)} %get-tuple-element.126.key_ref, bf16[1280,192]{1,0:T(8,128)(2,1)S(1)} %get-tuple-element.125.value_ref, f32[256,16]{1,0:T(8,128)S(1)} %copy-done.9, ...), custom_call_target="tpu_custom_call" | custom-call | tf_op jit(solution)/shard_map/attend_back/pallas_call | solution.py:196
  514.8 4.2 dynamic-slice_bitcast_fusion.1
  519.0 5.4 reshape.406
  524.4 7.9 constant_dynamic-slice_fusion.7
  553.2 4.4 fusion.55
  568.8 5.4 reshape.414
  574.2 4.3 dynamic-slice_bitcast_fusion
  578.5 18.5 %collective-permute-done.18 = bf16[384,576]{0,1:T(8,128)(2,1)S(1)} collective-permute-done((bf16[384,576]{0,1:T(8,128)(2,1)S(1)}, bf16[384,576]{0,1:T(8,128)(2,1)S(1)}, u32[]{:S(2)}, u32[]{:S(2)}) %collective-permute-start.18) | collective-permute-done | bytes 442400 | tf_op jit(solution)/shard_map/ppermute | solution.py:114
  600.6 11.3 %attend_back.3 = (f32[256,576]{1,0:T(8,128)S(1)}, f32[1280,384]{1,0:T(8,128)S(1)}) custom-call(bf16[256,576]{1,0:T(8,128)(2,1)S(1)} %copy.217.query_ref, bf16[1280,192]{1,0:T(8,128)(2,1)S(1)} %get-tuple-element.128.key_ref, bf16[1280,192]{1,0:T(8,128)(2,1)S(1)} %get-tuple-element.127.value_ref, f32[256,16]{1,0:T(8,128)S(1)} %get-tuple-element.49.total_ref, ...), custom_call_target="tpu_custom_call" | custom-call | tf_op jit(solution)/shard_map/attend_back/pallas_call | solution.py:196
  619.6 15.3 %collective-permute-done.22 = bf16[256,384]{1,0:T(8,128)(2,1)S(1)} collective-permute-done((bf16[256,384]{1,0:T(8,128)(2,1)S(1)}, bf16[256,384]{1,0:T(8,128)(2,1)S(1)}, u32[]{:S(2)}, u32[]{:S(2)}) %collective-permute-start.22) | collective-permute-done | bytes 196640 | tf_op jit(solution)/shard_map/ppermute | solution.py:523
  660.5 5.0 collective-permute-done.32
  677.6 28.4 %all-gather.24.cloned.1.call-done = bf16[2048,576]{1,0:T(8,128)(2,1)} async-done(((bf16[256,576]{1,0:T(8,128)(2,1)}), bf16[2048,576]{1,0:T(8,128)(2,1)}) %all-gather.24.cloned.1.call-update) | async-done | bytes 2359312 | tf_op jit(solution)/shard_map/all_gather | solution.py:552
  706.0 18.9 %fusion = f32[4000,576]{1,0:T(8,128)} fusion(bf16[2048,576]{1,0:T(8,128)(2,1)} %all-gather.24.cloned.1.call-done, s32[2048]{0:T(1024)S(1)} %bitcast.307), kind=kOutput, calls=%fused_computation.2 | convolution fusion | flops 9445376000 | bytes 11583488 | tf_op jit(solution)/shard_map/dot_general | solution.py:75
  724.9 11.8 %add.488 = f32[4000,576]{1,0:T(8,128)} add(f32[4000,576]{1,0:T(8,128)} %get-tuple-element.61, f32[4000,576]{1,0:T(8,128)} %fusion) | non-fusion elementwise | flops 2304000 | bytes 27648000 | tf_op jit(solution)/shard_map/add | solution.py:561
  736.7 8.8 constant_dynamic-slice_fusion.2
  745.5 5.7 copy.261
  759.5 5.4 collective-permute-done.24
  765.8 59.3 %all-reduce.11.cloned.1.call-done = (f32[144,3072]{1,0:T(8,128)}, f32[384,576]{0,1:T(8,128)}) async-done(((f32[144,3072]{1,0:T(8,128)}, f32[384,576]{0,1:T(8,128)}), (f32[144,3072]{1,0:T(8,128)}, f32[384,576]{0,1:T(8,128)})) %all-reduce.11.cloned.1.call-update) | async-done | bytes 2654224 | tf_op jit(solution)/shard_map/psum | solution.py:554
  841.0 6.0 copy.260
  847.1 4.9 bitcast_add_fusion
  857.9 138.7 %all-reduce.9.cloned.1.call-done = (f32[1,144,960]{2,1,0:T(8,128)}, f32[1,144,960]{2,1,0:T(8,128)}, f32[1,144,576]{2,1,0:T(8,128)}, f32[1,144,576]{2,1,0:T(8,128...) async-done(((f32[1,144,960]{2,1,0:T(8,128)}, f32[1,144,960]{2,1,0:T(8,128)}, f32[1,144,576]{2,1,0:T(8,128)}, f32[1,144,576]{2,1,0:T(8,128)}, f32[1,144,3072]{2,1,0:T(8,128)}, ...) | async-done | bytes 4423696 | tf_op jit(solution)/shard_map/psum | solution.py:557
  1017.9 3.6 collective-permute-done.43
  1032.1 3.7 add_multiply_fusion.3
  1037.3 12.2 %add_multiply_fusion = (f32[2,144,3072]{2,1,0:T(8,128)}, f32[2,144,3072]{2,1,0:T(8,128)}, f32[2,144,3072]{2,1,0:T(8,128)}) fusion(f32[2,144,3072]{2,1,0:T(8,128)} %param.39, f32[2,144,3072]{2,1,0:T(8,128)} %param.27, f32[]{:T(128)S(6)} %div.141, f32[1,144,3072]{2,1,0:T(8,128)} %bitcast.257, f32[1,144,3072]{2,1,0:T(8,128)} %get-tuple-element.81, ...), kind=kLoop, calls=%fused_computation.18 | loop fusion | flops 8847360 | bytes 24772612 | tf_op jit(solution)/shard_map/add | solution.py:320
  1049.6 5.5 add_multiply_fusion.2
  1055.8 5.3 add_multiply_fusion.1
  (551 shorter events, 267.9 us)
Async XLA Ops:
  7.2 54.8 %all-gather.38.cloned.1.call-start = ((), (), s32[]{:S(2)}) async-start(), calls=%async_computation.10 | async-start | bytes 5898240 | tf_op jit(solution)/shard_map/all_gather | solution.py:358
  10.1 138.8 %all-gather.26.cloned.1.call-start = ((), (), s32[]{:S(2)}) async-start(), calls=%async_computation.4 | async-start | bytes 1474560 | tf_op jit(solution)/shard_map/all_gather | solution.py:383
  12.6 164.8 %all-gather.28.cloned.1.call-start = ((), (), s32[]{:S(2)}) async-start(), calls=%async_computation.5 | async-start | bytes 4423680 | tf_op jit(solution)/shard_map/all_gather | solution.py:383
  14.2 169.6 %all-gather.30.cloned.1.call-start = ((), (), s32[]{:S(2)}) async-start(), calls=%async_computation.6 | async-start | bytes 2211840 | tf_op jit(solution)/shard_map/all_gather | solution.py:383
  16.1 171.3 %all-gather.32.cloned.1.call-start = ((), (), s32[]{:S(2)}) async-start(), calls=%async_computation.7 | async-start | bytes 1474560 | tf_op jit(solution)/shard_map/all_gather | solution.py:383
  16.7 217.8 %all-gather.34.cloned.1.call-start = ((), (), s32[]{:S(2)}) async-start(), calls=%async_computation.8 | async-start | bytes 4423680 | tf_op jit(solution)/shard_map/all_gather | solution.py:383
  86.5 58.3 %all-to-all-start = ((bf16[8,256,576]{1,2,0:T(8,128)(2,1)}), bf16[8,256,576]{1,2,0:T(8,128)(2,1)S(1)}, u32[]{:S(2)}, u32[]{:S(2)}) async-start(bf16[8,256,576]{1,2,0:T(8,128)(2,1)} %broadcast_select_fusion), calls=%async_computation | async-start | bytes 4718592 | tf_op jit(solution)/shard_map/all_to_all | solution.py:371
  90.3 151.0 %all-gather.36.cloned.1.call-start = ((), (), s32[]{:S(2)}) async-start(), calls=%async_computation.9 | async-start | bytes 2211840 | tf_op jit(solution)/shard_map/all_gather | solution.py:383
  91.0 216.3 %all-gather.22.cloned.1.call-start = ((), (), s32[]{:S(2)}) async-start(), calls=%async_computation.2 | async-start | bytes 2949120 | tf_op jit(solution)/shard_map/all_gather | solution.py:453
  152.6 12.6 %collective-permute-start = (bf16[256,384]{1,0:T(8,128)(2,1)S(1)}, bf16[256,384]{1,0:T(8,128)(2,1)}, u32[]{:S(2)}, u32[]{:S(2)}) collective-permute-start(bf16[256,384]{1,0:T(8,128)(2,1)S(1)} %pad_maximum_fusion.12), channel_id=1, source_target_pairs={{0,16},{4,20},{8,24},{12,28},{1,17},{5,21},{9,25},{13,29},{2,18},{... | collective-permute-start | bytes 589832 | tf_op jit(solution)/shard_map/ppermute | solution.py:411
  154.9 11.4 %collective-permute-start.1 = (bf16[256,384]{1,0:T(8,128)(2,1)S(1)}, bf16[256,384]{1,0:T(8,128)(2,1)}, u32[]{:S(2)}, u32[]{:S(2)}) collective-permute-start(bf16[256,384]{1,0:T(8,128)(2,1)S(1)} %pad_maximum_fusion.12), channel_id=1, source_target_pairs={{0,12},{4,16},{8,20},{12,24},{16,28},{1,13},{5,17},{9,21},{13,25},... | collective-permute-start | bytes 589832 | tf_op jit(solution)/shard_map/ppermute | solution.py:411
  160.7 7.6 collective-permute-start.2
  162.0 6.4 collective-permute-start.3
  192.9 24.7 %collective-permute-start.4 = (bf16[256,384]{1,0:T(8,128)(2,1)S(1)}, bf16[256,384]{1,0:T(8,128)(2,1)}, u32[]{:S(2)}, u32[]{:S(2)}) collective-permute-start(bf16[256,384]{1,0:T(8,128)(2,1)S(1)} %pad_maximum_fusion.13), channel_id=1, source_target_pairs={{0,16},{4,20},{8,24},{12,28},{1,17},{5,21},{9,25},{13,29},{2,18},{... | collective-permute-start | bytes 589832 | tf_op jit(solution)/shard_map/ppermute | solution.py:411
  210.4 8.9 collective-permute-start.5
  212.4 10.2 collective-permute-start.6
  214.5 9.0 collective-permute-start.7
  413.4 53.8 %all-to-all-start.1 = ((bf16[8,256,576]{1,2,0:T(8,128)(2,1)}), bf16[8,256,576]{1,2,0:T(8,128)(2,1)}, u32[]{:S(2)}, u32[]{:S(2)}) async-start(bf16[8,256,576]{1,2,0:T(8,128)(2,1)} %copy.230), calls=%async_computation.1 | async-start | bytes 4718592 | tf_op jit(solution)/shard_map/all_to_all | solution.py:472
  417.8 288.2 %all-gather.24.cloned.1.call-start = ((), (), s32[]{:S(2)}) async-start(), calls=%async_computation.3 | async-start | bytes 2949120 | tf_op jit(solution)/shard_map/all_gather | solution.py:552
  508.2 27.0 %collective-permute-start.14 = (bf16[256,384]{1,0:T(8,128)(2,1)}, bf16[256,384]{1,0:T(8,128)(2,1)S(1)}, u32[]{:S(2)}, u32[]{:S(2)}) collective-permute-start(bf16[256,384]{1,0:T(8,128)(2,1)} %get-tuple-element.122), channel_id=1, source_target_pairs={{16,0},{20,4},{24,8},{28,12},{17,1},{21,5},{25,9},{29,13},{18,2},{... | collective-permute-start | bytes 589832 | tf_op jit(solution)/shard_map/ppermute | solution.py:523
  509.5 26.2 %collective-permute-start.13 = (bf16[256,384]{1,0:T(8,128)(2,1)}, bf16[256,384]{1,0:T(8,128)(2,1)}, u32[]{:S(2)}, u32[]{:S(2)}) collective-permute-start(bf16[256,384]{1,0:T(8,128)(2,1)} %get-tuple-element.123), channel_id=1, source_target_pairs={{12,0},{16,4},{20,8},{24,12},{28,16},{13,1},{17,5},{21,9},{25,13},... | collective-permute-start | bytes 589832 | tf_op jit(solution)/shard_map/ppermute | solution.py:523
  510.8 25.0 %collective-permute-start.12 = (bf16[256,384]{1,0:T(8,128)(2,1)}, bf16[256,384]{1,0:T(8,128)(2,1)}, u32[]{:S(2)}, u32[]{:S(2)}) collective-permute-start(bf16[256,384]{1,0:T(8,128)(2,1)} %get-tuple-element.124), channel_id=1, source_target_pairs={{8,0},{12,4},{16,8},{20,12},{24,16},{28,20},{9,1},{13,5},{17,9},{2... | collective-permute-start | bytes 589832 | tf_op jit(solution)/shard_map/ppermute | solution.py:523
  512.1 23.7 %collective-permute-start.11 = (bf16[256,384]{1,0:T(8,128)(2,1)}, bf16[256,384]{1,0:T(8,128)(2,1)}, u32[]{:S(2)}, u32[]{:S(2)}) collective-permute-start(bf16[256,384]{1,0:T(8,128)(2,1)} %get-tuple-element.121), channel_id=1, source_target_pairs={{4,0},{8,4},{12,8},{16,12},{20,16},{24,20},{28,24},{5,1},{9,5},{13... | collective-permute-start | bytes 589832 | tf_op jit(solution)/shard_map/ppermute | solution.py:523
  519.0 40.3 %collective-permute-start.15 = (f32[2,144,3072]{2,1,0:T(8,128)}, f32[2,144,3072]{2,1,0:T(8,128)}, u32[]{:S(2)}, u32[]{:S(2)}) collective-permute-start(f32[2,144,3072]{2,1,0:T(8,128)} %dynamic-slice_bitcast_fusion.1), channel_id=1, source_target_pairs={{0,1},{1,0},{2,3},{3,2},{4,5},{5,4},{6,7},{7,6},{8,9},{9,8},{10,11... | collective-permute-start | bytes 10616840 | tf_op jit(solution)/shard_map/ppermute | solution.py:106
  535.2 22.4 %collective-permute-start.17 = (f32[2,384,576]{1,2,0:T(8,128)}, f32[2,384,576]{1,2,0:T(8,128)}, u32[]{:S(2)}, u32[]{:S(2)}) collective-permute-start(f32[2,384,576]{1,2,0:T(8,128)} %bitcast.233), channel_id=1, source_target_pairs={{0,1},{1,0},{2,3},{3,2},{4,5},{5,4},{6,7},{7,6},{8,9},{9,8},{10,11... | collective-permute-start | bytes 5308424 | tf_op jit(solution)/shard_map/ppermute | solution.py:106
  535.7 110.4 %collective-permute-start.33 = (f32[2,144,576]{2,1,0:T(8,128)}, f32[2,144,576]{2,1,0:T(8,128)}, u32[]{:S(2)}, u32[]{:S(2)}) collective-permute-start(f32[2,144,576]{2,1,0:T(8,128)} %dynamic-slice_bitcast_fusion.4), channel_id=1, source_target_pairs={{0,1},{1,0},{2,3},{3,2},{4,5},{5,4},{6,7},{7,6},{8,9},{9,8},{10,11... | collective-permute-start | bytes 1990664 | tf_op jit(solution)/shard_map/ppermute | solution.py:106
  565.3 32.7 %collective-permute-start.16 = (bf16[144,3072]{1,0:T(8,128)(2,1)}, bf16[144,3072]{1,0:T(8,128)(2,1)}, u32[]{:S(2)}, u32[]{:S(2)}) collective-permute-start(bf16[144,3072]{1,0:T(8,128)(2,1)} %fusion.31), channel_id=1, source_target_pairs={{0,2},{1,3},{2,0},{3,1},{4,6},{5,7},{6,4},{7,5},{8,10},{9,11},{10,... | collective-permute-start | bytes 2654216 | tf_op jit(solution)/shard_map/ppermute | solution.py:114
  566.9 30.1 %collective-permute-start.18 = (bf16[384,576]{0,1:T(8,128)(2,1)S(1)}, bf16[384,576]{0,1:T(8,128)(2,1)S(1)}, u32[]{:S(2)}, u32[]{:S(2)}) collective-permute-start(bf16[384,576]{0,1:T(8,128)(2,1)S(1)} %fusion.46), channel_id=1, source_target_pairs={{0,2},{1,3},{2,0},{3,1},{4,6},{5,7},{6,4},{7,5},{8,10},{9,11},{10,... | collective-permute-start | bytes 1327112 | tf_op jit(solution)/shard_map/ppermute | solution.py:114
  613.2 21.7 %collective-permute-start.22 = (bf16[256,384]{1,0:T(8,128)(2,1)S(1)}, bf16[256,384]{1,0:T(8,128)(2,1)S(1)}, u32[]{:S(2)}, u32[]{:S(2)}) collective-permute-start(bf16[256,384]{1,0:T(8,128)(2,1)S(1)} %get-tuple-element.118), channel_id=1, source_target_pairs={{16,0},{20,4},{24,8},{28,12},{17,1},{21,5},{25,9},{29,13},{18,2},{... | collective-permute-start | bytes 589832 | tf_op jit(solution)/shard_map/ppermute | solution.py:523
  614.5 20.4 %collective-permute-start.21 = (bf16[256,384]{1,0:T(8,128)(2,1)S(1)}, bf16[256,384]{1,0:T(8,128)(2,1)S(1)}, u32[]{:S(2)}, u32[]{:S(2)}) collective-permute-start(bf16[256,384]{1,0:T(8,128)(2,1)S(1)} %get-tuple-element.119), channel_id=1, source_target_pairs={{12,0},{16,4},{20,8},{24,12},{28,16},{13,1},{17,5},{21,9},{25,13},... | collective-permute-start | bytes 589832 | tf_op jit(solution)/shard_map/ppermute | solution.py:523
  615.8 19.6 %collective-permute-start.20 = (bf16[256,384]{1,0:T(8,128)(2,1)S(1)}, bf16[256,384]{1,0:T(8,128)(2,1)S(1)}, u32[]{:S(2)}, u32[]{:S(2)}) collective-permute-start(bf16[256,384]{1,0:T(8,128)(2,1)S(1)} %get-tuple-element.120), channel_id=1, source_target_pairs={{8,0},{12,4},{16,8},{20,12},{24,16},{28,20},{9,1},{13,5},{17,9},{2... | collective-permute-start | bytes 589832 | tf_op jit(solution)/shard_map/ppermute | solution.py:523
  617.1 18.4 %collective-permute-start.19 = (bf16[256,384]{1,0:T(8,128)(2,1)S(1)}, bf16[256,384]{1,0:T(8,128)(2,1)S(1)}, u32[]{:S(2)}, u32[]{:S(2)}) collective-permute-start(bf16[256,384]{1,0:T(8,128)(2,1)S(1)} %get-tuple-element.117), channel_id=1, source_target_pairs={{4,0},{8,4},{12,8},{16,12},{20,16},{24,20},{28,24},{5,1},{9,5},{13... | collective-permute-start | bytes 589832 | tf_op jit(solution)/shard_map/ppermute | solution.py:523
  634.9 14.8 %collective-permute-start.25 = (f32[2,144,576]{2,1,0:T(8,128)}, f32[2,144,576]{2,1,0:T(8,128)}, u32[]{:S(2)}, u32[]{:S(2)}) collective-permute-start(f32[2,144,576]{2,1,0:T(8,128)} %dynamic-slice_bitcast_fusion.5), channel_id=1, source_target_pairs={{0,1},{1,0},{2,3},{3,2},{4,5},{5,4},{6,7},{7,6},{8,9},{9,8},{10,11... | collective-permute-start | bytes 1990664 | tf_op jit(solution)/shard_map/ppermute | solution.py:106
  634.9 34.1 %collective-permute-start.27 = (f32[2,144,3072]{2,1,0:T(8,128)}, f32[2,144,3072]{2,1,0:T(8,128)}, u32[]{:S(2)}, u32[]{:S(2)}) collective-permute-start(f32[2,144,3072]{2,1,0:T(8,128)} %dynamic-slice_bitcast_fusion), channel_id=1, source_target_pairs={{0,1},{1,0},{2,3},{3,2},{4,5},{5,4},{6,7},{7,6},{8,9},{9,8},{10,11... | collective-permute-start | bytes 10616840 | tf_op jit(solution)/shard_map/ppermute | solution.py:106
  635.4 16.2 %collective-permute-start.31 = (f32[2,144,960]{2,1,0:T(8,128)}, f32[2,144,960]{2,1,0:T(8,128)}, u32[]{:S(2)}, u32[]{:S(2)}) collective-permute-start(f32[2,144,960]{2,1,0:T(8,128)} %dynamic-slice_bitcast_fusion.2), channel_id=1, source_target_pairs={{0,1},{1,0},{2,3},{3,2},{4,5},{5,4},{6,7},{7,6},{8,9},{9,8},{10,11... | collective-permute-start | bytes 3317768 | tf_op jit(solution)/shard_map/ppermute | solution.py:106
  642.4 182.6 %all-reduce.11.cloned.1.call-start = ((), (), s32[]{:S(2)}) async-start(), calls=%async_computation.12 | async-start | bytes 5308416 | tf_op jit(solution)/shard_map/psum | solution.py:554
  645.6 20.7 %collective-permute-start.29 = (f32[2,384,576]{1,2,0:T(8,128)S(1)}, f32[2,384,576]{1,2,0:T(8,128)S(1)}, u32[]{:S(2)}, u32[]{:S(2)}) collective-permute-start(f32[2,384,576]{1,2,0:T(8,128)S(1)} %bitcast.274), channel_id=1, source_target_pairs={{0,1},{1,0},{2,3},{3,2},{4,5},{5,4},{6,7},{7,6},{8,9},{9,8},{10,11... | collective-permute-start | bytes 5308424 | tf_op jit(solution)/shard_map/ppermute | solution.py:106
  648.2 7.6 collective-permute-start.34
  650.9 8.7 collective-permute-start.26
  653.3 12.2 %collective-permute-start.32 = (bf16[144,960]{1,0:T(8,128)(2,1)S(1)}, bf16[144,960]{1,0:T(8,128)(2,1)S(1)}, u32[]{:S(2)}, u32[]{:S(2)}) collective-permute-start(bf16[144,960]{1,0:T(8,128)(2,1)S(1)} %fusion.53), channel_id=1, source_target_pairs={{0,2},{1,3},{2,0},{3,1},{4,6},{5,7},{6,4},{7,5},{8,10},{9,11},{10,... | collective-permute-start | bytes 829448 | tf_op jit(solution)/shard_map/ppermute | solution.py:114
  667.5 83.8 %collective-permute-start.30 = (bf16[384,576]{0,1:T(8,128)(2,1)}, bf16[384,576]{0,1:T(8,128)(2,1)}, u32[]{:S(2)}, u32[]{:S(2)}) collective-permute-start(bf16[384,576]{0,1:T(8,128)(2,1)} %fusion.47), channel_id=1, source_target_pairs={{0,2},{1,3},{2,0},{3,1},{4,6},{5,7},{6,4},{7,5},{8,10},{9,11},{10,... | collective-permute-start | bytes 1327112 | tf_op jit(solution)/shard_map/ppermute | solution.py:114
  672.5 84.4 %collective-permute-start.28 = (bf16[144,3072]{1,0:T(8,128)(2,1)}, bf16[144,3072]{1,0:T(8,128)(2,1)}, u32[]{:S(2)}, u32[]{:S(2)}) collective-permute-start(bf16[144,3072]{1,0:T(8,128)(2,1)} %fusion.32), channel_id=1, source_target_pairs={{0,2},{1,3},{2,0},{3,1},{4,6},{5,7},{6,4},{7,5},{8,10},{9,11},{10,... | collective-permute-start | bytes 2654216 | tf_op jit(solution)/shard_map/ppermute | solution.py:114
  673.1 323.5 %all-reduce.9.cloned.1.call-start = ((), (), s32[]{:S(2)}) async-start(), calls=%async_computation.11 | async-start | bytes 9142272 | tf_op jit(solution)/shard_map/psum | solution.py:557
  677.6 75.9 %collective-permute-start.23 = (f32[2,144,960]{2,1,0:T(8,128)}, f32[2,144,960]{2,1,0:T(8,128)}, u32[]{:S(2)}, u32[]{:S(2)}) collective-permute-start(f32[2,144,960]{2,1,0:T(8,128)} %dynamic-slice_bitcast_fusion.3), channel_id=1, source_target_pairs={{0,1},{1,0},{2,3},{3,2},{4,5},{5,4},{6,7},{7,6},{8,9},{9,8},{10,11... | collective-permute-start | bytes 3317768 | tf_op jit(solution)/shard_map/ppermute | solution.py:106
  751.2 95.8 %collective-permute-start.40 = (f32[2,1000,576]{1,2,0:T(8,128)}, f32[2,1000,576]{1,2,0:T(8,128)}, u32[]{:S(2)}, u32[]{:S(2)}) collective-permute-start(f32[2,1000,576]{1,2,0:T(8,128)} %bitcast.263), channel_id=1, source_target_pairs={{0,1},{1,0},{2,3},{3,2},{4,5},{5,4},{6,7},{7,6},{8,9},{9,8},{10,11... | collective-permute-start | bytes 13824008 | tf_op jit(solution)/shard_map/ppermute | solution.py:106
  755.4 9.5 collective-permute-start.24
  839.6 17.7 %collective-permute-start.39 = (f32[5,576]{1,0:T(8,128)S(1)}, f32[5,576]{1,0:T(8,128)S(1)}, u32[]{:S(2)}, u32[]{:S(2)}) collective-permute-start(f32[5,576]{1,0:T(8,128)S(1)} %add.483), channel_id=1, source_target_pairs={{0,2},{1,3},{2,0},{3,1},{4,6},{5,7},{6,4},{7,5},{8,10},{9,11},{10,... | collective-permute-start | bytes 34568 | tf_op jit(solution)/shard_map/ppermute | solution.py:87
  855.3 154.8 %collective-permute-start.41 = (bf16[1000,576]{0,1:T(8,128)(2,1)}, bf16[1000,576]{0,1:T(8,128)(2,1)}, u32[]{:S(2)}, u32[]{:S(2)}) collective-permute-start(bf16[1000,576]{0,1:T(8,128)(2,1)} %fusion.30), channel_id=1, source_target_pairs={{0,2},{1,3},{2,0},{3,1},{4,6},{5,7},{6,4},{7,5},{8,10},{9,11},{10,... | collective-permute-start | bytes 3456008 | tf_op jit(solution)/shard_map/ppermute | solution.py:114
  (128 other events, 816.6 us)
Sparse Core Ops, SparseCore 0:
  10.2 40.6 all-gather.37
  53.1 17.4 all-gather.25
  72.7 30.8 all-gather.27
  105.6 21.2 all-gather.29
  128.8 17.8 all-gather.31
  148.7 30.7 all-gather.33
  181.6 20.7 all-gather.35
  246.2 61.1 all-gather.21
  642.5 63.4 all-gather.23
  710.1 114.8 all-reduce.10
  831.2 165.4 all-reduce.8
